TPU v7x, 32 devices: a whole 2x2x4 slice. The times are simulated.
32 devices in a mesh: bx: 4 (over z), by: 8 (over y, x, core).
Axes of the slice: x: 2, y: 2, z: 4, core: 2. Of those that a mesh axis runs over, the one named last changes fastest.
Arguments:
- state: float32 [384, 32, 1024], P(None, 'bx', 'by'), may hold values from -6 to 6
- target: bfloat16 [384, 32, 1024], P(None, 'bx', 'by'), may hold values from -6 to 6
- land_mask: int32 [32, 1024], P('bx', 'by'), may hold values 0 or 1
- batch_map: int32 [32, 1024], P('bx', 'by'), may hold values from 0 to 63
- diffusion: float32 [384], replicated, may hold values from 0.05 to 0.2
- speed_x: float32 [384], replicated, may hold values from -0.3 to 0.3
- speed_y: float32 [384], replicated, may hold values from -0.3 to 0.3
- w_in: bfloat16 [384, 4096], replicated, may hold values from -0.3125 to 0.3125
- w_out: bfloat16 [4096, 384], replicated, may hold values from -0.09375 to 0.09375
Outputs:
- new_state: float32 [384, 32, 1024], P(None, 'bx', 'by')
- grad_in: float32 [4096, 384], P(('bx', 'by'))
- grad_out: float32 [4096, 384], P(('bx', 'by'))
- batch_loss: float32 [64], replicated
All inputs are finite; a program needn't handle non-finite values. No bound on the sum of `land_mask` on one device may be relied on, other than what follows from the above.
Results may differ from a plain program's by a relative error of at most 0.0017.
Values sent between devices are 32-bit elements; how exact they have to be, the bound alone decides.
A program may use at most 128 MiB of HBM per device.

v0:
```python
import jax
import jax.numpy as jnp
from jax import lax
from jax.sharding import PartitionSpec as P

SUB = 3
BATCHES = 64


def extended(cells, sides, width):
    for axis, dim in sides:
        count = lax.axis_size(axis)
        ends = count - 1
        head = lax.slice_in_dim(cells, 0, width, axis=dim)
        tail = lax.slice_in_dim(cells, cells.shape[dim] - width, cells.shape[dim], axis=dim)
        cells = jnp.concatenate(
            [
                lax.ppermute(tail, axis, [(i, (i + 1) % count) for i in range(ends)]),
                cells,
                lax.ppermute(head, axis, [((i + 1) % count, i) for i in range(ends)]),
            ],
            axis=dim,
        )
    return cells


def advance(padded, kap, sxx, syy):
    centre = padded[:, 1:-1, 1:-1]
    east = padded[:, 2:, 1:-1]
    west = padded[:, :-2, 1:-1]
    north = padded[:, 1:-1, 2:]
    south = padded[:, 1:-1, :-2]
    return (
        centre
        + kap * (east + west + north + south - 4.0 * centre)
        - 0.5 * sxx * (east - west)
        - 0.5 * syy * (north - south)
    )


def on_device(state, target, land_mask, batch_map, diffusion, speed_x, speed_y, w_in, w_out):
    feats, rows_x, rows_y = state.shape
    kap = diffusion[:, None, None]
    sxx = speed_x[:, None, None]
    syy = speed_y[:, None, None]
    field = extended(state, (("bx", 1), ("by", 2)), SUB)
    for substep in range(SUB):
        field = advance(field, kap, sxx, syy)
        margin = SUB - substep - 1
        if margin > 0:
            along_x = (
                lax.axis_index("bx") * rows_x
                + jnp.arange(rows_x + 2 * margin, dtype=jnp.int32)
                - margin
            )
            along_y = (
                lax.axis_index("by") * rows_y
                + jnp.arange(rows_y + 2 * margin, dtype=jnp.int32)
                - margin
            )
            inside_x = ((along_x >= 0) & (along_x < rows_x * lax.axis_size("bx"))).astype(
                jnp.float32
            )
            inside_y = ((along_y >= 0) & (along_y < rows_y * lax.axis_size("by"))).astype(
                jnp.float32
            )
            field = field * inside_x[None, :, None] * inside_y[None, None, :]
    local_cols = rows_x * rows_y
    total = local_cols * lax.axis_size("bx") * lax.axis_size("by")
    inputs = field.reshape(feats, local_cols).T.astype(jnp.bfloat16)
    pre = jnp.dot(inputs, w_in, preferred_element_type=jnp.float32)
    hidden = jax.nn.silu(pre).astype(jnp.bfloat16)
    tend = jnp.dot(hidden, w_out, preferred_element_type=jnp.float32)
    weights = land_mask.reshape(local_cols).astype(jnp.float32)[:, None]
    err = weights * (tend - target.reshape(feats, local_cols).T.astype(jnp.float32))
    new_state = field + 0.5 * (weights * tend).T.reshape(feats, rows_x, rows_y)
    persq = 0.5 * jnp.sum(err * err, axis=1)
    onehot = (
        batch_map.reshape(local_cols)[:, None] == jnp.arange(BATCHES, dtype=jnp.int32)[None, :]
    ).astype(jnp.float32)
    partial_loss = jnp.dot(persq, onehot, precision=lax.Precision.HIGHEST) * (
        BATCHES / (total * feats)
    )
    batch_loss = lax.psum(partial_loss, ("bx", "by"))
    dtend = (err * total ** (-0.5)).astype(jnp.bfloat16)
    dhid = jnp.dot(dtend, w_out.T, preferred_element_type=jnp.float32)
    sig = jax.nn.sigmoid(pre)
    dpre = (dhid * sig * (1.0 + pre * (1.0 - sig))).astype(jnp.bfloat16)
    block = hidden
    grad_out = lax.psum_scatter(
        jnp.dot(block.T, dtend, preferred_element_type=jnp.float32),
        ("bx", "by"),
        scatter_dimension=0,
        tiled=True,
    )
    block = dpre
    grad_in = lax.psum_scatter(
        jnp.dot(block.T, inputs, preferred_element_type=jnp.float32),
        ("bx", "by"),
        scatter_dimension=0,
        tiled=True,
    )
    return (new_state, grad_in, grad_out, batch_loss)


def solution(mesh):
    placed = (
        P(None, "bx", "by"),
        P(None, "bx", "by"),
        P("bx", "by"),
        P("bx", "by"),
        P(),
        P(),
        P(),
        P(),
        P(),
    )
    return jax.shard_map(
        on_device,
        mesh=mesh,
        in_specs=placed,
        out_specs=(P(None, "bx", "by"), P(("bx", "by"), None), P(("bx", "by"), None), P()),
        check_vma=False,
    )
```

profile of v0, /device:TPU:0, one launch (start us, length us, event | category | flops | bytes accessed | tf_op | source)
XLA Modules:
  0.0 316.8 jit_solution(5757603913554681060)
XLA Ops:
  7.2 0.0 copy-start
  7.2 0.0 reduce-scatter.5.cloned.1.call-start
  7.2 2.3 fusion.9
  9.5 0.9 copy.25
  10.4 5.8 %collective-permute-start = (f32[384,3,128]{2,0,1:T(8,128)}, f32[384,3,128]{2,0,1:T(8,128)}, u32[]{:S(2)}, u32[]{:S(2)}) collective-permute-start(f32[384,3,128]{2,0,1:T(8,128)} %copy.25), channel_id=1, source_target_pairs={{0,8},{8,16},{16,24},{1,9},{9,17},{17,25},{2,10},{10,18},{18,26},{... | collective-permute-start | bytes 1769480 | tf_op jit(solution)/shard_map/ppermute | solution.py:18
  16.1 0.9 copy.26
  17.0 1.3 collective-permute-start.1
  18.3 0.0 copy-start.6
  18.4 0.0 copy-start.7
  18.4 0.0 copy-start.8
  18.4 3.1 copy.18
  21.4 2.9 copy.23
  24.3 0.0 copy-done.6
  24.3 0.0 copy-done.7
  24.3 0.0 copy-done.8
  24.3 3.9 %collective-permute-done = f32[384,3,128]{2,0,1:T(8,128)} collective-permute-done((f32[384,3,128]{2,0,1:T(8,128)}, f32[384,3,128]{2,0,1:T(8,128)}, u32[]{:S(2)}, u32[]{:S(2)}) %collective-permute-start) | collective-permute-done | bytes 589856 | tf_op jit(solution)/shard_map/ppermute | solution.py:18
  28.2 2.2 copy.17
  30.5 3.5 %collective-permute-done.1 = f32[384,3,128]{2,0,1:T(8,128)} collective-permute-done((f32[384,3,128]{2,0,1:T(8,128)}, f32[384,3,128]{2,0,1:T(8,128)}, u32[]{:S(2)}, u32[]{:S(2)}) %collective-permute-start.1) | collective-permute-done | bytes 589856 | tf_op jit(solution)/shard_map/ppermute | solution.py:20
  34.0 2.3 copy.19
  36.3 2.4 pad_maximum_fusion
  38.7 1.3 collective-permute-start.2
  40.0 1.3 collective-permute-start.3
  41.3 0.9 copy.21
  42.2 0.0 collective-permute-done.2
  42.2 2.6 collective-permute-done.3
  44.9 0.0 copy-start.5
  44.9 0.2 pad_maximum_fusion.1
  45.1 0.4 copy-done.5
  45.6 1.9 multiply_multiply_fusion
  47.5 1.3 multiply_multiply_fusion.1
  48.8 2.1 fusion.7
  50.9 0.0 copy-start.3
  50.9 0.0 copy-done
  50.9 0.0 copy-start.2
  50.9 0.0 copy-start.9
  50.9 9.1 %multiply_convert_fusion.1 = (bf16[1024,4096]{1,0:T(8,128)(2,1)S(1)}, f32[1024,4096]{1,0:T(8,128)}) fusion(bf16[384,1024]{0,1:T(8,128)(2,1)S(1)} %bitcast.29, bf16[384,4096]{1,0:T(8,128)(2,1)S(1)} %copy-done), kind=kOutput, calls=%fused_computation.1 | convolution fusion | flops 3242196992 | bytes 29097984 | tf_op jit(solution)/shard_map/dot_general | solution.py:71
  60.0 0.0 copy-done.3
  60.0 0.0 copy-done.2
  60.0 0.0 copy-done.9
  60.0 5.7 %multiply_reduce_fusion = (f32[1024]{0:T(1024)S(1)}, f32[1024,384]{1,0:T(8,128)S(1)}, f32[1024,384]{1,0:T(8,128)}) fusion(f32[384,8,128]{0,2,1:T(8,128)S(1)} %copy-done.2, f32[1024]{0:T(1024)S(1)} %convert_bitcast_fusion, bf16[1024,4096]{1,0:T(8,128)(2,1)S(1)} %get-tuple-element.17, bf16[4096,384]{1,0:T(8,128)(2,1)S(1)} %copy-done.9), kind=kOutput, calls=%fused_computation.9 | convolution fusion | flops 3223583744 | bytes 16261120 | tf_op jit(solution)/shard_map/dot_general | solution.py:73
  65.7 6.5 %fusion.2 = f32[4096,384]{1,0:T(8,128)} fusion(bf16[1024,4096]{1,0:T(8,128)(2,1)S(1)} %get-tuple-element.17, f32[1024,384]{1,0:T(8,128)S(1)} %get-tuple-element.9), kind=kOutput, calls=%fused_computation.16 | convolution fusion | flops 3222011904 | bytes 16252928 | tf_op jit(solution)/shard_map/dot_general | solution.py:91
  72.2 0.0 reduce-scatter.5.cloned.1.call-update
  72.2 0.0 reduce-scatter.3.cloned.1.call-start
  72.3 0.0 copy-start.4
  72.3 11.9 %multiply_convert_fusion = bf16[1024,4096]{1,0:T(8,128)(2,1)S(1)} fusion(f32[1024,4096]{1,0:T(8,128)} %get-tuple-element.18, bf16[4096,384]{1,0:T(8,128)(2,1)} %param.17, f32[1024,384]{1,0:T(8,128)S(1)} %get-tuple-element.9), kind=kOutput, calls=%fused_computation | convolution fusion | flops 3259760640 | bytes 29884416 | tf_op jit(solution)/shard_map/dot_general | solution.py:86
  84.2 0.0 copy-done.4
  84.2 6.5 %fusion.10 = f32[4096,384]{1,0:T(8,128)} fusion(bf16[1024,4096]{1,0:T(8,128)(2,1)S(1)} %multiply_convert_fusion, bf16[384,1024]{0,1:T(8,128)(2,1)S(1)} %bitcast.30), kind=kOutput, calls=%fused_computation.31 | convolution fusion | flops 3221225472 | bytes 15466496 | tf_op jit(solution)/shard_map/dot_general | solution.py:98
  90.7 0.0 reduce-scatter.3.cloned.1.call-update
  90.7 0.0 copy-start.1
  90.7 3.4 %add.134 = f32[384,8,128]{0,2,1:T(8,128)} add(f32[384,8,128]{0,2,1:T(8,128)} %get-tuple-element.11, f32[384,8,128]{0,2,1:T(8,128)} %bitcast.28) | non-fusion elementwise | flops 393216 | bytes 4718592 | tf_op jit(solution)/shard_map/add | solution.py:76
  94.2 0.0 copy-start.10
  94.2 3.1 copy.24
  97.3 0.0 copy-done.10
  97.3 0.4 fusion.1
  97.6 43.1 %psum.7 = f32[64]{0:T(128)} all-reduce(f32[64]{0:T(128)S(1)} %fusion.1), channel_id=1, replica_groups=mesh['bx'=4,'by'=8] {'bx','by'}, use_global_device_ids=true, to_apply=%region_3.4 | all-reduce | flops 64 | bytes 512 | tf_op jit(solution)/shard_map/psum | solution.py:84
  140.8 49.1 %reduce-scatter.5.cloned.1.call-done = f32[128,384]{1,0:T(8,128)} async-done(((f32[4096,384]{1,0:T(8,128)}), f32[128,384]{1,0:T(8,128)}) %reduce-scatter.5.cloned.1.call-update) | async-done | bytes 196624 | tf_op jit(solution)/shard_map/reduce_scatter | solution.py:90
  189.9 120.1 %reduce-scatter.3.cloned.1.call-done = f32[128,384]{1,0:T(8,128)} async-done(((f32[4096,384]{1,0:T(8,128)}), f32[128,384]{1,0:T(8,128)}) %reduce-scatter.3.cloned.1.call-update) | async-done | bytes 196624 | tf_op jit(solution)/shard_map/reduce_scatter | solution.py:97
  310.0 0.0 copy-done.1
  (10 shorter events, 0.1 us)
Async XLA Ops:
  7.2 43.7 %copy-start = (bf16[384,4096]{1,0:T(8,128)(2,1)S(1)}, bf16[384,4096]{1,0:T(8,128)(2,1)}, u32[]{:S(2)}) copy-start(bf16[384,4096]{1,0:T(8,128)(2,1)} %param.16) | copy-start | bytes 9437188
  7.2 182.7 %reduce-scatter.5.cloned.1.call-start = ((), (), s32[]{:S(2)}) async-start(), calls=%async_computation.3 | async-start | bytes 6488064 | tf_op jit(solution)/shard_map/reduce_scatter | solution.py:90
  10.4 17.8 %collective-permute-start = (f32[384,3,128]{2,0,1:T(8,128)}, f32[384,3,128]{2,0,1:T(8,128)}, u32[]{:S(2)}, u32[]{:S(2)}) collective-permute-start(f32[384,3,128]{2,0,1:T(8,128)} %copy.25), channel_id=1, source_target_pairs={{0,8},{8,16},{16,24},{1,9},{9,17},{17,25},{2,10},{10,18},{18,26},{... | collective-permute-start | bytes 1769480 | tf_op jit(solution)/shard_map/ppermute | solution.py:18
  17.0 17.0 %collective-permute-start.1 = (f32[384,3,128]{2,0,1:T(8,128)}, f32[384,3,128]{2,0,1:T(8,128)}, u32[]{:S(2)}, u32[]{:S(2)}) collective-permute-start(f32[384,3,128]{2,0,1:T(8,128)} %copy.26), channel_id=1, source_target_pairs={{8,0},{16,8},{24,16},{9,1},{17,9},{25,17},{10,2},{18,10},{26,18},{... | collective-permute-start | bytes 1769480 | tf_op jit(solution)/shard_map/ppermute | solution.py:20
  18.3 6.0 %copy-start.6 = (s32[8,128]{1,0:T(8,128)S(1)}, s32[8,128]{1,0:T(8,128)}, u32[]{:S(2)}) copy-start(s32[8,128]{1,0:T(8,128)} %param.11) | copy-start | bytes 12292
  18.4 6.0 %copy-start.7 = (f32[384]{0:T(512)S(1)}, f32[384]{0:T(512)}, u32[]{:S(2)}) copy-start(f32[384]{0:T(512)} %param.15) | copy-start | bytes 4612
  18.4 6.0 %copy-start.8 = (f32[384]{0:T(512)S(1)}, f32[384]{0:T(512)}, u32[]{:S(2)}) copy-start(f32[384]{0:T(512)} %param.14) | copy-start | bytes 4612
  38.7 3.5 %collective-permute-start.2 = (f32[384,14,3]{0,1,2:T(8,128)S(1)}, f32[384,14,3]{0,1,2:T(8,128)S(1)}, u32[]{:S(2)}, u32[]{:S(2)}) collective-permute-start(f32[384,14,3]{0,1,2:T(8,128)S(1)} %get-tuple-element.12), channel_id=1, source_target_pairs={{0,1},{1,2},{2,3},{3,4},{4,5},{5,6},{6,7},{8,9},{9,10},{10,11},{11... | collective-permute-start | bytes 193544 | tf_op jit(solution)/shard_map/ppermute | solution.py:18
  40.0 4.9 %collective-permute-start.3 = (f32[384,14,3]{0,1,2:T(8,128)S(1)}, f32[384,14,3]{0,1,2:T(8,128)S(1)}, u32[]{:S(2)}, u32[]{:S(2)}) collective-permute-start(f32[384,14,3]{0,1,2:T(8,128)S(1)} %get-tuple-element.13), channel_id=1, source_target_pairs={{1,0},{2,1},{3,2},{4,3},{5,4},{6,5},{7,6},{9,8},{10,9},{11,10},{12... | collective-permute-start | bytes 193544 | tf_op jit(solution)/shard_map/ppermute | solution.py:20
  44.9 0.7 copy-start.5
  50.9 9.1 %copy-start.3 = (bf16[384,8,128]{0,2,1:T(8,128)(2,1)}, bf16[384,8,128]{0,2,1:T(8,128)(2,1)S(1)}, u32[]{:S(2)}) copy-start(bf16[384,8,128]{0,2,1:T(8,128)(2,1)S(1)} %get-tuple-element.10) | copy-start | bytes 2359300
  50.9 9.1 %copy-start.2 = (f32[384,8,128]{0,2,1:T(8,128)S(1)}, f32[384,8,128]{0,2,1:T(8,128)}, u32[]{:S(2)}) copy-start(f32[384,8,128]{0,2,1:T(8,128)} %copy.23) | copy-start | bytes 4718596
  50.9 9.1 %copy-start.9 = (bf16[4096,384]{1,0:T(8,128)(2,1)S(1)}, bf16[4096,384]{1,0:T(8,128)(2,1)}, u32[]{:S(2)}) copy-start(bf16[4096,384]{1,0:T(8,128)(2,1)} %param.17) | copy-start | bytes 9437188
  72.2 237.8 %reduce-scatter.3.cloned.1.call-start = ((), (), s32[]{:S(2)}) async-start(), calls=%async_computation.2 | async-start | bytes 6488064 | tf_op jit(solution)/shard_map/reduce_scatter | solution.py:97
  72.3 11.9 %copy-start.4 = (bf16[384,8,128]{0,2,1:T(8,128)(2,1)S(1)}, bf16[384,8,128]{0,2,1:T(8,128)(2,1)}, u32[]{:S(2)}) copy-start(bf16[384,8,128]{0,2,1:T(8,128)(2,1)} %copy-done.3) | copy-start | bytes 2359300
  90.7 219.3 %copy-start.1 = (bf16[384,4096]{1,0:T(8,128)(2,1)S(1)}, bf16[384,4096]{1,0:T(8,128)(2,1)}, u32[]{:S(2)}) copy-start(bf16[384,4096]{1,0:T(8,128)(2,1)} %param.16) | copy-start | bytes 9437188
  94.2 3.1 copy-start.10
Sparse Core Ops, SparseCore 0:
  72.3 117.5 reduce-scatter.4
  196.1 113.8 reduce-scatter.2
where the time goes:
time: 317 us
  waiting for transfers between devices  179 us (56%)
  blocking collectives  43.1 us (14%)
  matrix products  40 us (13%)
  local copies, waits for them, and re-layouts  19 us (6%)
  between operations  14.3 us (5%)
  other arithmetic  11.4 us (4%)
  starting transfers between devices  9.7 us (3%)
    reduce_scatter x1, waiting for transfers between devices, on_device(): lax.psum_scatter(jnp.dot(block.T, inputs, preferred_element_type=jnp.floa...  120 us
    reduce_scatter x1, waiting for transfers between devices, on_device(): lax.psum_scatter(jnp.dot(block.T, dtend, preferred_element_type=jnp.float...  49.1 us
    psum x1, blocking collectives, on_device(): batch_loss = lax.psum(partial_loss, ('bx', 'by'))  43.1 us
    dot_general x1, matrix products, on_device(): dhid = jnp.dot(dtend, w_out.T, preferred_element_type=jnp.float32)  11.9 us
    dot_general x1, matrix products, on_device(): pre = jnp.dot(inputs, w_in, preferred_element_type=jnp.float32)  9.1 us
    unnamed x26, local copies, waits for them, and re-layouts  8.36 us
    ppermute x2, starting transfers between devices, extended(): lax.ppermute(tail, axis, [(i, (i + 1) % count) for i in range(ends)])  7.05 us
    dot_general x1, matrix products, on_device(): jnp.dot(block.T, inputs, preferred_element_type=jnp.float32)  6.48 us
  transfers between devices with their start and end apart: 6, of which 5 were waited for; matrix products, arithmetic and copies ran while one was open for 11% of the time, Pallas kernels for 0%

commit v1 on v0

v1 whole, which is shorter than its diff:
```python
import functools

import jax
import jax.numpy as jnp
from jax import lax
from jax.experimental import pallas as pl
from jax.experimental.pallas import tpu as pltpu
from jax.sharding import PartitionSpec as P

SUB = 3
BATCHES = 64
CHUNKS = 4
MESH = pl.DeviceIdType.MESH
F32 = jnp.float32
BF16 = jnp.bfloat16


def extended(cells, sides, width):
    for axis, dim in sides:
        count = lax.axis_size(axis)
        ends = count - 1
        head = lax.slice_in_dim(cells, 0, width, axis=dim)
        tail = lax.slice_in_dim(cells, cells.shape[dim] - width, cells.shape[dim], axis=dim)
        cells = jnp.concatenate(
            [
                lax.ppermute(tail, axis, [(i, (i + 1) % count) for i in range(ends)]),
                cells,
                lax.ppermute(head, axis, [((i + 1) % count, i) for i in range(ends)]),
            ],
            axis=dim,
        )
    return cells


def advance(padded, kap, sxx, syy):
    centre = padded[:, 1:-1, 1:-1]
    east = padded[:, 2:, 1:-1]
    west = padded[:, :-2, 1:-1]
    north = padded[:, 1:-1, 2:]
    south = padded[:, 1:-1, :-2]
    return (
        centre
        + kap * (east + west + north + south - 4.0 * centre)
        - 0.5 * sxx * (east - west)
        - 0.5 * syy * (north - south)
    )


def transported(state, diffusion, speed_x, speed_y):
    feats, rows_x, rows_y = state.shape
    kap = diffusion[:, None, None]
    sxx = speed_x[:, None, None]
    syy = speed_y[:, None, None]
    field = extended(state, (("bx", 1), ("by", 2)), SUB)
    for substep in range(SUB):
        field = advance(field, kap, sxx, syy)
        margin = SUB - substep - 1
        if margin > 0:
            along_x = (
                lax.axis_index("bx") * rows_x
                + jnp.arange(rows_x + 2 * margin, dtype=jnp.int32)
                - margin
            )
            along_y = (
                lax.axis_index("by") * rows_y
                + jnp.arange(rows_y + 2 * margin, dtype=jnp.int32)
                - margin
            )
            inside_x = ((along_x >= 0) & (along_x < rows_x * lax.axis_size("bx"))).astype(F32)
            inside_y = ((along_y >= 0) & (along_y < rows_y * lax.axis_size("by"))).astype(F32)
            field = field * inside_x[None, :, None] * inside_y[None, None, :]
    return field


def tree(parts):
    if len(parts) == 1:
        return parts[0]
    return tree(parts[::2]) + tree(parts[1::2])


def backward_kernel(
    zs, bs, gathered,
    x_ref, xt_ref, d_ref, dt_ref, wi_ref, wo_ref, loss_ref,
    gin_ref, gout_ref, total_ref,
    g0, g1, c0, c1, q0, q1, a0, a1, z0, z1, lc, lq, la, lz,
    send, recv, lsend, lrecv,
):
    quads = bs // 4
    me_z, me_b = lax.axis_index("bx"), lax.axis_index("by")
    core, q, a = lax.rem(me_b, 2), lax.rem(me_b // 2, 2), me_b // 4
    rows, feats = g0.shape[-2:]
    grads, cores, qs, quadss, zz = (g0, g1), (c0, c1), (q0, q1), (a0, a1), (z0, z1)
    outs = (gout_ref, gin_ref)

    def other_a(s):
        return lax.rem(a + s, quads)

    def other_z(s):
        return lax.rem(me_z + s, zs)

    core_peer = (me_z, me_b + 1 - 2 * core)
    q_peer = (me_z, me_b + 2 - 4 * q)
    a_peers = [(me_z, other_a(s) * 4 + lax.rem(me_b, 4)) for s in range(1, quads)]
    z_peers = [(other_z(s), me_b) for s in range(1, zs)]
    everyone = [core_peer, q_peer] + a_peers + z_peers

    barrier = pltpu.get_barrier_semaphore()
    for peer in everyone:
        pl.semaphore_signal(barrier, inc=1, device_id=peer, device_id_type=MESH)

    def remote(src, dst, peer, ssem, rsem):
        return pltpu.make_async_remote_copy(
            src_ref=src, dst_ref=dst, send_sem=ssem, recv_sem=rsem,
            device_id=peer, device_id_type=MESH,
        )

    kq, ka, kz = 1, 2, 2 + quads - 1

    def copies(stage, m, c):
        def one(src, dst, peer, k):
            return remote(src, dst, peer, send.at[c, m, k], recv.at[c, m, k])

        if stage == 0:
            return [one(grads[m].at[c, :, :, :, 1 - core], cores[m].at[c], core_peer, 0)]
        if stage == 3:
            held = a0.at[c, 0] if m == 0 else q1.at[c]
            return [
                one(held.at[other_z(s)], zz[m].at[c, s - 1], z_peers[s - 1], kz + s - 1)
                for s in range(1, zs)
            ]
        if (m == 0) == (stage == 1):
            src = c0.at[c, :, :, 1 - q] if m == 0 else a1.at[c, 0, :, 1 - q]
            return [one(src, qs[m].at[c], q_peer, kq)]
        held = q0 if m == 0 else c1
        return [
            one(held.at[c, :, other_a(s)], quadss[m].at[c, s - 1], a_peers[s - 1], ka + s - 1)
            for s in range(1, quads)
        ]

    def gather_sum(stage, m, c):
        if stage == 0:
            @pl.loop(0, zs)
            def _(z):
                cores[m][c, z] = cores[m][c, z] + grads[m][c, z, :, :, core]
        elif stage == 3:
            own = a0[c, 0, me_z] if m == 0 else q1[c, me_z]
            outs[m][c * rows:(c + 1) * rows] = tree(
                [own] + [zz[m][c, s] for s in range(zs - 1)]
            )
        elif (m == 0) == (stage == 1):
            own = c0[c, :, :, q] if m == 0 else a1[c, 0, :, q]
            qs[m][c] = qs[m][c] + own
        else:
            own = q0[c, :, a] if m == 0 else c1[c, :, a]
            quadss[m][c, 0] = tree([own] + [quadss[m][c, s] for s in range(quads - 1)])

    def loss_copies(stage):
        if stage == 0:
            return [remote(loss_ref, lc, core_peer, lsend.at[0], lrecv.at[0])]
        if stage == 1:
            return [remote(lc, lq, q_peer, lsend.at[1], lrecv.at[1])]
        if stage == 2:
            return [
                remote(lq, la.at[s - 1], a_peers[s - 1], lsend.at[ka + s - 1], lrecv.at[ka + s - 1])
                for s in range(1, quads)
            ]
        return [
            remote(la.at[0], lz.at[s - 1], z_peers[s - 1], lsend.at[kz + s - 1], lrecv.at[kz + s - 1])
            for s in range(1, zs)
        ]

    def loss_sum(stage):
        if stage == 0:
            lc[...] = lc[...] + loss_ref[...]
        elif stage == 1:
            lq[...] = lq[...] + lc[...]
        elif stage == 2:
            la[0] = tree([lq[...]] + [la[s] for s in range(quads - 1)])
        else:
            total_ref[...] = tree([la[0]] + [lz[s] for s in range(zs - 1)])

    def compute(c):
        @pl.loop(0, zs)
        def _(z):
            if gathered:
                wi = wi_ref[pl.ds(z * bs, bs), c].reshape(bs * rows, feats)
                wo = wo_ref[pl.ds(z * bs, bs), c].reshape(bs * rows, feats)
            else:
                wi, wo = wi_ref[c * zs + z], wo_ref[c * zs + z]
            pre = jnp.dot(wi, xt_ref[...], preferred_element_type=F32)
            sig = jax.nn.sigmoid(pre)
            hidden = (pre * sig).astype(BF16)
            g0[c, z] = jnp.dot(hidden, d_ref[...], preferred_element_type=F32).reshape(
                quads, 2, 2, rows, feats
            )
            dhid = jnp.dot(wo, dt_ref[...], preferred_element_type=F32)
            dpre = (dhid * sig * (1.0 + pre * (1.0 - sig))).astype(BF16)
            g1[c, z] = jnp.dot(dpre, x_ref[...], preferred_element_type=F32).reshape(
                quads, 2, 2, rows, feats
            )

    started = []

    def begin(group):
        for copy in group:
            copy.start()
            started.append(copy)
        return group

    flying = {}
    for step in range(CHUNKS + 4):
        if step < CHUNKS:
            compute(step)
            if step == 0:
                pl.semaphore_wait(barrier, len(everyone))
            for m in range(2):
                flying[0, m, step] = begin(copies(0, m, step))
        if step == 0:
            flying["loss", 0] = begin(loss_copies(0))
        for stage in range(4):
            c = step - 1 - stage
            if not 0 <= c < CHUNKS:
                continue
            for m in range(2):
                for copy in flying[stage, m, c]:
                    copy.wait_recv()
                gather_sum(stage, m, c)
                if stage < 3:
                    flying[stage + 1, m, c] = begin(copies(stage + 1, m, c))
            if c == 0:
                for copy in flying["loss", stage]:
                    copy.wait_recv()
                if stage == 2:
                    loss_sum(stage)
                    flying["loss", 3] = begin(loss_copies(3))
                else:
                    loss_sum(stage)
                    if stage < 3:
                        flying["loss", stage + 1] = begin(loss_copies(stage + 1))
    for copy in started:
        copy.wait_send()


def backward(x, xt, d, dt, wi, wo, partial_loss):
    zs, bs = lax.axis_size("bx"), lax.axis_size("by")
    quads = bs // 4
    hid, feats = wo.shape
    blocks = zs * bs
    rows = hid // blocks // CHUNKS
    gathered = rows % 16 == 0
    wi = wi.T.reshape(blocks, CHUNKS, rows, feats)
    wo = wo.reshape(blocks, CHUNKS, rows, feats)
    if not gathered:
        wi, wo = (
            w.transpose(1, 0, 2, 3).reshape(CHUNKS * zs, bs * rows, feats) for w in (wi, wo)
        )
    kinds = 2 + (quads - 1) + (zs - 1)
    vmem = pl.BlockSpec(memory_space=pltpu.VMEM)
    tile = partial_loss.shape

    def buf(*shape):
        return pltpu.VMEM((CHUNKS,) + shape + (rows, feats), F32)

    grad = jax.ShapeDtypeStruct((rows * CHUNKS, feats), F32)
    return pl.pallas_call(
        functools.partial(backward_kernel, zs, bs, gathered),
        out_shape=(grad, grad, jax.ShapeDtypeStruct(tile, F32)),
        in_specs=[vmem] * 7,
        out_specs=(vmem,) * 3,
        scratch_shapes=[
            buf(zs, quads, 2, 2), buf(zs, quads, 2, 2),
            buf(zs, quads, 2), buf(zs, quads, 2),
            buf(zs, quads), buf(zs),
            buf(quads - 1, zs), buf(quads - 1, zs, 2),
            buf(zs - 1), buf(zs - 1),
            pltpu.VMEM(tile, F32), pltpu.VMEM(tile, F32),
            pltpu.VMEM((quads - 1,) + tile, F32), pltpu.VMEM((zs - 1,) + tile, F32),
            pltpu.SemaphoreType.DMA((CHUNKS, 2, kinds)),
            pltpu.SemaphoreType.DMA((CHUNKS, 2, kinds)),
            pltpu.SemaphoreType.DMA((kinds,)),
            pltpu.SemaphoreType.DMA((kinds,)),
        ],
        compiler_params=pltpu.CompilerParams(collective_id=0, has_side_effects=True),
    )(x, xt, d, dt, wi, wo, partial_loss)


def on_device(state, target, land_mask, batch_map, diffusion, speed_x, speed_y, w_in, w_out):
    feats, rows_x, rows_y = state.shape
    field = transported(state, diffusion, speed_x, speed_y)
    local_cols = rows_x * rows_y
    total = local_cols * lax.axis_size("bx") * lax.axis_size("by")
    flat = field.reshape(feats, local_cols)
    xt = flat.astype(BF16)
    x = xt.T
    pre = jnp.dot(x, w_in, preferred_element_type=F32)
    hidden = jax.nn.silu(pre).astype(BF16)
    tend = jnp.dot(hidden, w_out, preferred_element_type=F32).T
    weights = land_mask.reshape(local_cols).astype(F32)[None, :]
    err = weights * (tend - target.reshape(feats, local_cols).astype(F32))
    new_state = (flat + 0.5 * (weights * tend)).reshape(feats, rows_x, rows_y)
    persq = 0.5 * jnp.sum(err * err, axis=0)
    width = -(-BATCHES // 128) * 128
    onehot = (
        batch_map.reshape(local_cols)[:, None] == jnp.arange(width, dtype=jnp.int32)[None, :]
    ).astype(F32)
    partial_loss = jnp.dot(persq, onehot, precision=lax.Precision.HIGHEST) * (
        BATCHES / (total * feats)
    )
    dt = (err * total ** (-0.5)).astype(BF16)
    grad_in, grad_out, loss = backward(
        x, xt, dt.T, dt, w_in, w_out, jnp.broadcast_to(partial_loss[None, :], (8, width))
    )
    return (new_state, grad_in, grad_out, loss[0, :BATCHES])


def solution(mesh):
    placed = (
        P(None, "bx", "by"),
        P(None, "bx", "by"),
        P("bx", "by"),
        P("bx", "by"),
        P(),
        P(),
        P(),
        P(),
        P(),
    )
    return jax.shard_map(
        on_device,
        mesh=mesh,
        in_specs=placed,
        out_specs=(P(None, "bx", "by"), P(("bx", "by"), None), P(("bx", "by"), None), P()),
        check_vma=False,
    )
```

time: 317 us -> 154 us (0.49)
  waiting for transfers between devices: 179 us -> 5.5 us
  Pallas kernels: 0 us -> 89.2 us
  blocking collectives: 43.1 us -> 0 us
  matrix products: 40 us -> 15.8 us
  between operations: 14.3 us -> 0.86 us
  local copies, waits for them, and re-layouts: 19 us -> 23.6 us
    reduce_scatter x2 -> x0, waiting for transfers between devices: 169 us -> none  [the longest x1 120 us: on_device(): lax.psum_scatter(jnp.dot(block.T, inputs, preferred_element_type=jnp.floa...]
    pallas_call x0 -> x1, Pallas kernels: none -> 89.2 us  [backward(): pl.pallas_call(functools.partial(backward_kernel, zs, bs, gathered), out_...]
    psum x1 -> x0, blocking collectives: 43.1 us -> none  [on_device(): batch_loss = lax.psum(partial_loss, ('bx', 'by'))]
    dot_general x5 -> x1, matrix products: 39.7 us -> 15.4 us  [on_device(): tend = jnp.dot(hidden, w_out, preferred_element_type=F32).T]
    transpose x0 -> x3, local copies, waits for them, and re-layouts: none -> 7.07 us  [the longest x1 4.71 us: backward(): wi = wi.T.reshape(blocks, CHUNKS, rows, feats)]
    add x1 -> x0, other arithmetic: 3.45 us -> none  [on_device(): new_state = field + 0.5 * (weights * tend).T.reshape(feats, rows_x, rows_y)]
    ppermute x2, waiting for transfers between devices: 3.89 us -> 0.64 us  [extended(): lax.ppermute(tail, axis, [(i, (i + 1) % count) for i in range(ends)])]
    unnamed x26 -> x22, local copies, waits for them, and re-layouts: 8.36 us -> 8.32 us
  transfers between devices with their start and end apart: 6 -> 4, of which waited for: 5 -> 3; matrix products, arithmetic and copies ran while one was open for 11% -> 7% of each run, Pallas kernels for 0% -> 0%
where the time goes in v1:
time: 154 us
  Pallas kernels  89.2 us (58%)
  local copies, waits for them, and re-layouts  23.6 us (15%)
  matrix products  15.8 us (10%)
  starting transfers between devices  10.3 us (7%)
  other arithmetic  8.72 us (6%)
  waiting for transfers between devices  5.5 us (4%)
    pallas_call x1, Pallas kernels, backward(): pl.pallas_call(functools.partial(backward_kernel, zs, bs, gathered), out_...  89.2 us
    dot_general x1, matrix products, on_device(): tend = jnp.dot(hidden, w_out, preferred_element_type=F32).T  15.4 us
    unnamed x22, local copies, waits for them, and re-layouts  8.32 us
    ppermute x2, starting transfers between devices, extended(): lax.ppermute(tail, axis, [(i, (i + 1) % count) for i in range(ends)])  7.72 us
    ppermute x2, waiting for transfers between devices, extended(): lax.ppermute(head, axis, [((i + 1) % count, i) for i in range(ends)])  4.86 us
    transpose x1, local copies, waits for them, and re-layouts, backward(): wi = wi.T.reshape(blocks, CHUNKS, rows, feats)  4.71 us
    mul x2, other arithmetic, transported(): field = field * inside_x[None, :, None] * inside_y[None, None, :]  3.42 us
  transfers between devices with their start and end apart: 4, of which 3 were waited for; matrix products, arithmetic and copies ran while one was open for 7% of the time, Pallas kernels for 0%

profile of v1, /device:TPU:0, one launch (start us, length us, event | category | flops | bytes accessed | tf_op | source)
XLA Modules:
  0.0 153.8 jit_solution(7106899882680052378)
XLA Ops:
  0.6 2.2 %fusion.11 = (f32[384,3,128]{2,1,0:T(4,128)S(1)}, f32[384,3,128]{2,1,0:T(4,128)S(1)}) fusion(f32[384,8,128]{2,1,0:T(8,128)} %param.9), kind=kLoop, calls=%fused_computation.31 | loop fusion | bytes 2359296 | tf_op jit(solution)/shard_map/slice | solution.py:23
  2.8 0.0 copy-start
  2.8 0.9 copy.33
  3.7 1.3 collective-permute-start.1
  4.9 0.9 copy.32
  5.8 6.4 %collective-permute-start = (f32[384,3,128]{2,0,1:T(8,128)}, f32[384,3,128]{2,0,1:T(8,128)}, u32[]{:S(2)}, u32[]{:S(2)}) collective-permute-start(f32[384,3,128]{2,0,1:T(8,128)} %copy.32), channel_id=1, source_target_pairs={{0,8},{8,16},{16,24},{1,9},{9,17},{17,25},{2,10},{10,18},{18,26},{... | collective-permute-start | bytes 1769480 | tf_op jit(solution)/shard_map/ppermute | solution.py:26
  12.2 0.0 copy-done
  12.3 0.7 copy.20
  12.9 2.5 %convert.1 = f32[48,8,8,128]{3,2,1,0:T(8,128)} convert(bf16[48,8,8,128]{3,2,1,0:T(8,128)(2,1)} %bitcast.53) | non-fusion elementwise | flops 393216 | bytes 2359296
  15.4 0.0 copy-start.4
  15.4 0.0 copy-start.5
  15.4 0.0 copy-start.6
  15.4 4.7 %copy.27 = bf16[4096,384]{1,0:T(8,128)(2,1)} copy(bf16[4096,384]{0,1:T(8,128)(2,1)} %bitcast.50) | data formatting | bytes 6291456 | tf_op jit(solution)/shard_map/transpose | solution.py:251
  20.1 0.0 copy-done.4
  20.1 0.0 copy-done.5
  20.1 0.0 copy-done.6
  20.2 2.1 %collective-permute-done.1 = f32[384,3,128]{2,0,1:T(8,128)} collective-permute-done((f32[384,3,128]{2,0,1:T(8,128)}, f32[384,3,128]{2,0,1:T(8,128)}, u32[]{:S(2)}, u32[]{:S(2)}) %collective-permute-start.1) | collective-permute-done | bytes 589856 | tf_op jit(solution)/shard_map/ppermute | solution.py:28
  22.2 1.4 copy.21
  23.6 0.6 collective-permute-done
  24.3 1.4 copy.19
  25.7 0.5 pad_maximum_fusion
  26.2 1.3 collective-permute-start.2
  27.5 1.3 collective-permute-start.3
  28.9 0.9 copy.23
  29.7 0.0 collective-permute-done.2
  29.8 2.8 %collective-permute-done.3 = f32[384,14,3]{0,1,2:T(8,128)S(1)} collective-permute-done((f32[384,14,3]{0,1,2:T(8,128)S(1)}, f32[384,14,3]{0,1,2:T(8,128)S(1)}, u32[]{:S(2)}, u32[]{:S(2)}) %collective-permute-start.3) | collective-permute-done | bytes 64544 | tf_op jit(solution)/shard_map/ppermute | solution.py:28
  32.6 0.0 copy-start.3
  32.6 0.2 pad_maximum_fusion.1
  32.9 0.4 copy-done.3
  33.3 2.1 %multiply_multiply_fusion = f32[384,12,132]{0,2,1:T(8,128)S(1)} fusion(f32[384,14,134]{0,2,1:T(8,128)S(1)} %pad_maximum_fusion.1, f32[132]{0:T(256)S(1)} %and_convert_fusion.2, f32[12]{0:T(128)S(1)} %and_convert_fusion.3, f32[384]{0:T(512)S(1)} %get-tuple-element.17, f32[384]{0:T(512)S(1)} %get-tuple-element.18, f32[384]{0:T(512)S(1)} %copy-done.3), kind=kLoop, calls=%fused_computation.5 | loop fusion | flops 9123840 | bytes 14603328 | tf_op jit(solution)/shard_map/mul | solution.py:71
  35.4 1.3 multiply_multiply_fusion.1
  36.7 0.9 multiply_subtract_fusion
  37.6 0.5 copy.31
  38.1 0.1 convert_bitcast_fusion.1
  38.2 1.0 convert_element_type.60.xt_ref
  39.2 1.2 copy.28.x_ref
  40.4 15.4 %multiply_reduce_fusion = (f32[1024]{0:T(1024)S(1)}, bf16[384,1024]{1,0:T(8,128)(2,1)S(1)}, f32[48,8,8,128]{3,1,2,0:T(8,128)}) fusion(f32[48,8,8,128]{3,2,1,0:T(8,128)} %convert.1, f32[1024]{0:T(1024)S(1)} %convert_bitcast_fusion, f32[384,1024]{1,0:T(8,128)S(1)} %copy.31, bf16[4096,384]{1,0:T(8,128)(2,1)} %param.17, bf16[384,4096]{1,0:T(8,128)(2,1)} %param.16), kind=kOutput, calls=%fused_computation.13 | convolution fusion | flops 6467353600 | bytes 11804672 | tf_op jit(solution)/shard_map/dot_general | solution.py:297
  55.8 0.0 copy-start.1
  55.8 0.0 copy-start.2
  55.8 0.0 copy-start.7
  55.8 1.2 copy.29.d_ref
  57.0 0.8 copy-done.2
  57.8 1.5 copy.34
  59.3 0.0 copy-done.1
  59.3 0.0 copy-done.7
  59.3 0.4 fusion.7
  59.6 0.6 broadcast_in_dim.2.loss_ref
  60.3 89.2 %shard_map.120 = (f32[128,384]{1,0:T(8,128)}, f32[128,384]{1,0:T(8,128)}, f32[8,128]{1,0:T(8,128)}) custom-call(bf16[1024,384]{1,0:T(8,128)(2,1)} %copy.28.x_ref, bf16[384,1024]{1,0:T(8,128)(2,1)} %convert_element_type.60.xt_ref, bf16[1024,384]{1,0:T(8,128)(2,1)} %copy.29.d_ref, bf16[384,1024]{1,0:T(8,128)(2,1)} %copy-done.1, ...), custom_call_target="tpu_custom_call" | custom-call | tf_op jit(solution)/shard_map/pallas_call | solution.py:265
  149.4 1.2 slice_bitcast_fusion
  150.6 1.6 %copy.43 = f32[128,384]{1,0:T(8,128)} copy(f32[128,384]{1,0:T(8,128)} %get-tuple-element.24) | data formatting | bytes 393216
  152.2 1.6 %copy.44 = f32[128,384]{1,0:T(8,128)} copy(f32[128,384]{1,0:T(8,128)} %get-tuple-element.25) | data formatting | bytes 393216
  (10 shorter events, 0.1 us)
Async XLA Ops:
  2.8 9.5 %copy-start = (f32[384,8,128]{2,1,0:T(8,128)S(1)}, f32[384,8,128]{2,1,0:T(8,128)}, u32[]{:S(2)}) copy-start(f32[384,8,128]{2,1,0:T(8,128)} %param.9) | copy-start | bytes 4718596
  3.7 18.6 %collective-permute-start.1 = (f32[384,3,128]{2,0,1:T(8,128)}, f32[384,3,128]{2,0,1:T(8,128)}, u32[]{:S(2)}, u32[]{:S(2)}) collective-permute-start(f32[384,3,128]{2,0,1:T(8,128)} %copy.33), channel_id=1, source_target_pairs={{8,0},{16,8},{24,16},{9,1},{17,9},{25,17},{10,2},{18,10},{26,18},{... | collective-permute-start | bytes 1769480 | tf_op jit(solution)/shard_map/ppermute | solution.py:28
  5.8 18.5 %collective-permute-start = (f32[384,3,128]{2,0,1:T(8,128)}, f32[384,3,128]{2,0,1:T(8,128)}, u32[]{:S(2)}, u32[]{:S(2)}) collective-permute-start(f32[384,3,128]{2,0,1:T(8,128)} %copy.32), channel_id=1, source_target_pairs={{0,8},{8,16},{16,24},{1,9},{9,17},{17,25},{2,10},{10,18},{18,26},{... | collective-permute-start | bytes 1769480 | tf_op jit(solution)/shard_map/ppermute | solution.py:26
  15.4 4.7 %copy-start.4 = (s32[8,128]{1,0:T(8,128)S(1)}, s32[8,128]{1,0:T(8,128)}, u32[]{:S(2)}) copy-start(s32[8,128]{1,0:T(8,128)} %param.11) | copy-start | bytes 12292
  15.4 4.7 %copy-start.5 = (f32[384]{0:T(512)S(1)}, f32[384]{0:T(512)}, u32[]{:S(2)}) copy-start(f32[384]{0:T(512)} %param.15) | copy-start | bytes 4612
  15.4 4.7 %copy-start.6 = (f32[384]{0:T(512)S(1)}, f32[384]{0:T(512)}, u32[]{:S(2)}) copy-start(f32[384]{0:T(512)} %param.14) | copy-start | bytes 4612
  26.2 3.5 %collective-permute-start.2 = (f32[384,14,3]{0,1,2:T(8,128)S(1)}, f32[384,14,3]{0,1,2:T(8,128)S(1)}, u32[]{:S(2)}, u32[]{:S(2)}) collective-permute-start(f32[384,14,3]{0,1,2:T(8,128)S(1)} %get-tuple-element.12), channel_id=1, source_target_pairs={{0,1},{1,2},{2,3},{3,4},{4,5},{5,6},{6,7},{8,9},{9,10},{10,11},{11... | collective-permute-start | bytes 193544 | tf_op jit(solution)/shard_map/ppermute | solution.py:26
  27.5 5.0 %collective-permute-start.3 = (f32[384,14,3]{0,1,2:T(8,128)S(1)}, f32[384,14,3]{0,1,2:T(8,128)S(1)}, u32[]{:S(2)}, u32[]{:S(2)}) collective-permute-start(f32[384,14,3]{0,1,2:T(8,128)S(1)} %get-tuple-element.13), channel_id=1, source_target_pairs={{1,0},{2,1},{3,2},{4,3},{5,4},{6,5},{7,6},{9,8},{10,9},{11,10},{12... | collective-permute-start | bytes 193544 | tf_op jit(solution)/shard_map/ppermute | solution.py:28
  32.6 0.7 copy-start.3
  55.8 3.5 %copy-start.1 = (bf16[384,1024]{1,0:T(8,128)(2,1)}, bf16[384,1024]{1,0:T(8,128)(2,1)S(1)}, u32[]{:S(2)}) copy-start(bf16[384,1024]{1,0:T(8,128)(2,1)S(1)} %get-tuple-element.11.dt_ref) | copy-start | bytes 2359300
  55.8 2.0 %copy-start.2 = (f32[48,8,8,128]{3,1,2,0:T(8,128)S(1)}, f32[48,8,8,128]{3,1,2,0:T(8,128)}, u32[]{:S(2)}) copy-start(f32[48,8,8,128]{3,1,2,0:T(8,128)} %get-tuple-element.14) | copy-start | bytes 4718596
  55.8 3.4 %copy-start.7 = (s32[8,128]{1,0:T(8,128)S(1)}, s32[8,128]{1,0:T(8,128)}, u32[]{:S(2)}) copy-start(s32[8,128]{1,0:T(8,128)} %param.12) | copy-start | bytes 12292

commit v2 on v1

--- a/solution.py
+++ b/solution.py
@@ -15,61 +15,134 @@
 BF16 = jnp.bfloat16
 
 
-def extended(cells, sides, width):
-    for axis, dim in sides:
-        count = lax.axis_size(axis)
-        ends = count - 1
-        head = lax.slice_in_dim(cells, 0, width, axis=dim)
-        tail = lax.slice_in_dim(cells, cells.shape[dim] - width, cells.shape[dim], axis=dim)
-        cells = jnp.concatenate(
-            [
-                lax.ppermute(tail, axis, [(i, (i + 1) % count) for i in range(ends)]),
-                cells,
-                lax.ppermute(head, axis, [((i + 1) % count, i) for i in range(ends)]),
-            ],
-            axis=dim,
+WIDE = 8
+EDGE = 2 * WIDE
+SIDES = [(dx, dy) for dx in (-1, 0, 1) for dy in (-1, 0, 1) if dx or dy]
+
+
+def halo_kernel(zs, bs, cells, coef, out, first, second, send, recv):
+    rows, depth, feats = cells.shape
+    me_z, me_b = lax.axis_index("bx"), lax.axis_index("by")
+    window = pl.ds(EDGE, depth)
+
+    def has(side):
+        dx, dy = side
+        found = []
+        if dx:
+            found.append(me_z > 0 if dx < 0 else me_z < zs - 1)
+        if dy:
+            found.append(me_b > 0 if dy < 0 else me_b < bs - 1)
+        return functools.reduce(jnp.logical_and, found)
+
+    for buf in (first, second):
+        for i in range(rows + 2 * SUB):
+            buf[i, :EDGE] = jnp.zeros((EDGE, feats), F32)
+            buf[i, EDGE + depth:] = jnp.zeros((EDGE, feats), F32)
+    for i in list(range(SUB)) + list(range(rows + SUB, rows + 2 * SUB)):
+        first[i, window] = jnp.zeros((depth, feats), F32)
+
+    barrier = pltpu.get_barrier_semaphore()
+    for dx, dy in SIDES:
+        @pl.when(has((dx, dy)))
+        def _():
+            pl.semaphore_signal(
+                barrier, inc=1, device_id=(me_z + dx, me_b + dy), device_id_type=MESH
+            )
+    near_z = jnp.where(me_z > 0, 1, 0) + jnp.where(me_z < zs - 1, 1, 0)
+    near_b = jnp.where(me_b > 0, 1, 0) + jnp.where(me_b < bs - 1, 1, 0)
+    pl.semaphore_wait(barrier, near_z + near_b + near_z * near_b)
+
+    def own(side):
+        dx, dy = side
+        i = {-1: pl.ds(0, SUB), 0: pl.ds(0, rows), 1: pl.ds(rows - SUB, SUB)}[dx]
+        j = {-1: pl.ds(0, WIDE), 0: pl.ds(0, depth), 1: pl.ds(depth - WIDE, WIDE)}[dy]
+        return cells.at[i, j]
+
+    def slot(side):
+        dx, dy = side
+        i = {-1: pl.ds(0, SUB), 0: pl.ds(SUB, rows), 1: pl.ds(SUB + rows, SUB)}[dx]
+        j = {-1: pl.ds(WIDE, WIDE), 0: window, 1: pl.ds(EDGE + depth, WIDE)}[dy]
+        return first.at[i, j]
+
+    def copy_to(side):
+        dx, dy = side
+        back = (-dx, -dy)
+        return pltpu.make_async_remote_copy(
+            src_ref=own(side), dst_ref=slot(back),
+            send_sem=send.at[SIDES.index(side)], recv_sem=recv.at[SIDES.index(back)],
+            device_id=(me_z + dx, me_b + dy), device_id_type=MESH,
         )
-    return cells
-
-
-def advance(padded, kap, sxx, syy):
-    centre = padded[:, 1:-1, 1:-1]
-    east = padded[:, 2:, 1:-1]
-    west = padded[:, :-2, 1:-1]
-    north = padded[:, 1:-1, 2:]
-    south = padded[:, 1:-1, :-2]
-    return (
-        centre
-        + kap * (east + west + north + south - 4.0 * centre)
-        - 0.5 * sxx * (east - west)
-        - 0.5 * syy * (north - south)
+
+    for side in sorted(SIDES, key=lambda s: (s[1] != 0, s[0] == 0)):
+        @pl.when(has(side))
+        def _():
+            copy_to(side).start()
+    for i in range(rows):
+        first[SUB + i, window] = cells[i]
+    for side in SIDES:
+        @pl.when(has(side))
+        def _():
+            copy_to((-side[0], -side[1])).wait_recv()
+    for side in SIDES:
+        @pl.when(has(side))
+        def _():
+            copy_to(side).wait_send()
+
+    kap, sxx, syy = coef[0:1], coef[1:2], coef[2:3]
+    low = jnp.where(me_b > 0, 1.0, 0.0).astype(F32)
+    high = jnp.where(me_b < bs - 1, 1.0, 0.0).astype(F32)
+
+    def moved(src, i, start, count):
+        centre = src[i, pl.ds(start, count)]
+        east = src[i + 1, pl.ds(start, count)]
+        west = src[i - 1, pl.ds(start, count)]
+        north = src[i, pl.ds(start + 1, count)]
+        south = src[i, pl.ds(start - 1, count)]
+        return (
+            centre
+            + kap * (east + west + north + south - 4.0 * centre)
+            - 0.5 * sxx * (east - west)
+            - 0.5 * syy * (north - south)
+        )
+
+    for step in range(SUB):
+        src, dst = ((first, second), (second, first))[step % 2]
+        margin = SUB - step - 1
+
+        @pl.loop(SUB - margin, SUB + rows + margin)
+        def _(i):
+            if margin == 0:
+                out[i - SUB] = moved(src, i, EDGE, depth)
+            else:
+                at = me_z * rows + i - SUB
+                inside = jnp.where((at >= 0) & (at < rows * zs), 1.0, 0.0).astype(F32)
+                dst[i, pl.ds(WIDE, WIDE)] = moved(src, i, WIDE, WIDE) * (inside * low)
+                dst[i, window] = moved(src, i, EDGE, depth) * inside
+                dst[i, pl.ds(EDGE + depth, WIDE)] = moved(src, i, EDGE + depth, WIDE) * (
+                    inside * high
+                )
+
+
+def transported(state, diffusion, speed_x, speed_y):
+    zs, bs = lax.axis_size("bx"), lax.axis_size("by")
+    cells = state.transpose(1, 2, 0)
+    rows, depth, feats = cells.shape
+    coef = jnp.concatenate(
+        [jnp.stack([diffusion, speed_x, speed_y]), jnp.zeros((5, feats), F32)], axis=0
     )
-
-
-def transported(state, diffusion, speed_x, speed_y):
-    feats, rows_x, rows_y = state.shape
-    kap = diffusion[:, None, None]
-    sxx = speed_x[:, None, None]
-    syy = speed_y[:, None, None]
-    field = extended(state, (("bx", 1), ("by", 2)), SUB)
-    for substep in range(SUB):
-        field = advance(field, kap, sxx, syy)
-        margin = SUB - substep - 1
-        if margin > 0:
-            along_x = (
-                lax.axis_index("bx") * rows_x
-                + jnp.arange(rows_x + 2 * margin, dtype=jnp.int32)
-                - margin
-            )
-            along_y = (
-                lax.axis_index("by") * rows_y
-                + jnp.arange(rows_y + 2 * margin, dtype=jnp.int32)
-                - margin
-            )
-            inside_x = ((along_x >= 0) & (along_x < rows_x * lax.axis_size("bx"))).astype(F32)
-            inside_y = ((along_y >= 0) & (along_y < rows_y * lax.axis_size("by"))).astype(F32)
-            field = field * inside_x[None, :, None] * inside_y[None, None, :]
-    return field
+    vmem = pl.BlockSpec(memory_space=pltpu.VMEM)
+    padded = pltpu.VMEM((rows + 2 * SUB, depth + 2 * EDGE, feats), F32)
+    return pl.pallas_call(
+        functools.partial(halo_kernel, zs, bs),
+        out_shape=jax.ShapeDtypeStruct(cells.shape, F32),
+        in_specs=[vmem] * 2,
+        out_specs=vmem,
+        scratch_shapes=[
+            padded, padded,
+            pltpu.SemaphoreType.DMA((len(SIDES),)), pltpu.SemaphoreType.DMA((len(SIDES),)),
+        ],
+        compiler_params=pltpu.CompilerParams(collective_id=1, has_side_effects=True),
+    )(cells, coef)
 
 
 def tree(parts):
@@ -289,16 +362,16 @@
     field = transported(state, diffusion, speed_x, speed_y)
     local_cols = rows_x * rows_y
     total = local_cols * lax.axis_size("bx") * lax.axis_size("by")
-    flat = field.reshape(feats, local_cols)
-    xt = flat.astype(BF16)
-    x = xt.T
+    flat = field.reshape(local_cols, feats)
+    x = flat.astype(BF16)
+    xt = x.T
     pre = jnp.dot(x, w_in, preferred_element_type=F32)
     hidden = jax.nn.silu(pre).astype(BF16)
-    tend = jnp.dot(hidden, w_out, preferred_element_type=F32).T
-    weights = land_mask.reshape(local_cols).astype(F32)[None, :]
-    err = weights * (tend - target.reshape(feats, local_cols).astype(F32))
-    new_state = (flat + 0.5 * (weights * tend)).reshape(feats, rows_x, rows_y)
-    persq = 0.5 * jnp.sum(err * err, axis=0)
+    tend = jnp.dot(hidden, w_out, preferred_element_type=F32)
+    weights = land_mask.reshape(local_cols).astype(F32)[:, None]
+    err = weights * (tend - target.reshape(feats, local_cols).T.astype(F32))
+    new_state = (flat + 0.5 * (weights * tend)).T.reshape(feats, rows_x, rows_y)
+    persq = 0.5 * jnp.sum(err * err, axis=1)
     width = -(-BATCHES // 128) * 128
     onehot = (
         batch_map.reshape(local_cols)[:, None] == jnp.arange(width, dtype=jnp.int32)[None, :]
@@ -306,9 +379,9 @@
     partial_loss = jnp.dot(persq, onehot, precision=lax.Precision.HIGHEST) * (
         BATCHES / (total * feats)
     )
-    dt = (err * total ** (-0.5)).astype(BF16)
+    d = (err * total ** (-0.5)).astype(BF16)
     grad_in, grad_out, loss = backward(
-        x, xt, dt.T, dt, w_in, w_out, jnp.broadcast_to(partial_loss[None, :], (8, width))
+        x, xt, d, d.T, w_in, w_out, jnp.broadcast_to(partial_loss[None, :], (8, width))
     )
     return (new_state, grad_in, grad_out, loss[0, :BATCHES])
 

time: 154 us -> 155 us (level)
  Pallas kernels: 89.2 us -> 112 us
  starting transfers between devices: 10.3 us -> 0 us
  waiting for transfers between devices: 5.5 us -> 0 us
  local copies, waits for them, and re-layouts: 23.6 us -> 19.6 us
  other arithmetic: 8.72 us -> 6.43 us
    pallas_call x0 -> x1, Pallas kernels: none -> 27.4 us  [transported(): pl.pallas_call(functools.partial(halo_kernel, zs, bs), out_shape=jax.Shap...]
    ppermute x4 -> x0, starting transfers between devices: 10.3 us -> none  [the longest x2 7.72 us: extended(): lax.ppermute(tail, axis, [(i, (i + 1) % count) for i in range(ends)])]
    ppermute x4 -> x0, waiting for transfers between devices: 5.5 us -> none  [the longest x2 4.86 us: extended(): lax.ppermute(head, axis, [((i + 1) % count, i) for i in range(ends)])]
    pallas_call x1, Pallas kernels: 89.2 us -> 84.1 us  [backward(): pl.pallas_call(functools.partial(backward_kernel, zs, bs, gathered), out_...]
    convert_element_type x0 -> x2, local copies, waits for them, and re-layouts: none -> 4.77 us  [the longest x1 2.49 us: on_device(): d = (err * total ** (-0.5)).astype(BF16)]
    reduce_sum x0 -> x1, other arithmetic: none -> 3.55 us  [on_device(): persq = 0.5 * jnp.sum(err * err, axis=1)]
    mul x4 -> x1, other arithmetic: 3.43 us -> 0.01 us  [on_device(): persq = 0.5 * jnp.sum(err * err, axis=1)]
    ppermute x4 -> x0, local copies, waits for them, and re-layouts: 2.83 us -> none  [the longest x2 1.42 us: extended(): lax.ppermute(tail, axis, [(i, (i + 1) % count) for i in range(ends)])]
  transfers between devices with their start and end apart: 4 -> 0, of which waited for: 3 -> 0; matrix products, arithmetic and copies ran while one was open for 7% -> 0% of each run, Pallas kernels for 0% -> 0%
where the time goes in v2:
time: 155 us; the launch traced here: 154 us
  Pallas kernels  112 us (72%)
  local copies, waits for them, and re-layouts  19.6 us (13%)
  matrix products  16 us (10%)
  other arithmetic  6.43 us (4%)
    pallas_call x1, Pallas kernels, backward(): pl.pallas_call(functools.partial(backward_kernel, zs, bs, gathered), out_...  84.1 us
    pallas_call x1, Pallas kernels, transported(): pl.pallas_call(functools.partial(halo_kernel, zs, bs), out_shape=jax.Shap...  27.4 us
    dot_general x1, matrix products, on_device(): tend = jnp.dot(hidden, w_out, preferred_element_type=F32)  15.6 us
    unnamed x22, local copies, waits for them, and re-layouts  6.47 us
    transpose x1, local copies, waits for them, and re-layouts, backward(): wi = wi.T.reshape(blocks, CHUNKS, rows, feats)  4.63 us
    reduce_sum x1, other arithmetic, on_device(): persq = 0.5 * jnp.sum(err * err, axis=1)  3.55 us

profile of v2, /device:TPU:0, one launch (start us, length us, event | category | flops | bytes accessed | tf_op | source)
XLA Modules:
  0.0 154.3 jit_solution(10115095462709164613)
XLA Ops:
  0.6 0.0 copy-start.5
  0.6 0.0 copy-start.6
  0.7 0.0 copy-start.7
  0.7 3.0 %copy.13 = f32[384,8,128]{0,2,1:T(8,128)} copy(f32[384,8,128]{2,1,0:T(8,128)} %param.9) | data formatting | bytes 3145728 | tf_op args[0]
  3.7 0.0 copy-done.5
  3.7 0.0 copy-done.6
  3.7 0.0 copy-done.7
  3.8 0.1 pad.3.clone
  3.8 0.7 maximum_maximum_fusion.coef
  4.5 27.4 %shard_map.120 = f32[8,128,384]{2,1,0:T(8,128)} custom-call(f32[8,128,384]{2,1,0:T(8,128)} %bitcast.57, f32[8,384]{1,0:T(8,128)} %maximum_maximum_fusion.coef), custom_call_target="tpu_custom_call" | custom-call | tf_op jit(solution)/shard_map/pallas_call | solution.py:135
  31.9 1.9 %copy.22 = f32[1024,384]{0,1:T(8,128)S(1)} copy(f32[1024,384]{1,0:T(8,128)} %bitcast.58) | data formatting | bytes 3145728 | tf_op jit(solution)/shard_map/reshape | solution.py:365
  33.8 0.0 copy-start.1
  33.8 1.0 convert_element_type.37
  34.8 0.0 copy-start.4
  34.8 0.3 copy-done.1
  35.2 0.2 convert.3
  35.3 0.2 copy-done.4
  35.6 0.0 copy-start
  35.6 15.6 %fusion.7 = (bf16[384,1024]{1,0:T(8,128)(2,1)}, f32[1024,384]{0,1:T(8,128)}) fusion(f32[48,8,8,128]{3,2,1,0:T(8,128)S(1)} %convert.3, f32[1024]{0:T(1024)S(1)} %convert_bitcast_fusion, bf16[4096,384]{1,0:T(8,128)(2,1)} %param.17, bf16[1024,384]{0,1:T(8,128)(2,1)} %convert_element_type.37, bf16[384,4096]{1,0:T(8,128)(2,1)} %param.16), kind=kOutput, calls=%fused_computation.9 | convolution fusion | flops 6464995328 | bytes 11014144 | tf_op jit(solution)/shard_map/dot_general | solution.py:370
  51.2 0.0 copy-done
  51.2 3.5 %multiply_reduce_fusion = (f32[1024]{0:T(1024)S(1)}, bf16[1024,384]{0,1:T(8,128)(2,1)}, f32[48,8,8,128]{3,1,2,0:T(8,128)S(1)}) fusion(f32[1024,384]{0,1:T(8,128)} %get-tuple-element.14, f32[48,8,8,128]{3,2,1,0:T(8,128)} %copy-done, f32[1024]{0:T(1024)S(1)} %convert_bitcast_fusion, f32[1024,384]{0,1:T(8,128)S(1)} %copy.22), kind=kLoop, calls=%fused_computation.10 | loop fusion | flops 3537920 | bytes 7086080 | tf_op jit(solution)/shard_map/reduce_sum | solution.py:374
  54.7 0.0 copy-start.8
  54.7 2.5 %copy.20.d_ref = bf16[1024,384]{1,0:T(8,128)(2,1)} copy(bf16[1024,384]{0,1:T(8,128)(2,1)} %get-tuple-element.11) | data formatting | bytes 1572864 | tf_op jit(solution)/shard_map/convert_element_type | solution.py:382
  57.2 0.0 copy-done.8
  57.2 0.4 fusion.8
  57.6 0.6 broadcast_in_dim.5.loss_ref
  58.2 2.3 %copy.19.x_ref = bf16[1024,384]{1,0:T(8,128)(2,1)} copy(bf16[1024,384]{0,1:T(8,128)(2,1)} %convert_element_type.37) | data formatting | bytes 1572864 | tf_op jit(solution)/shard_map/convert_element_type | solution.py:366
  60.5 1.0 convert_bitcast_fusion.1.xt_ref
  61.5 4.6 %copy.18 = bf16[4096,384]{1,0:T(8,128)(2,1)} copy(bf16[4096,384]{0,1:T(8,128)(2,1)} %bitcast.59) | data formatting | bytes 6291456 | tf_op jit(solution)/shard_map/transpose | solution.py:324
  66.2 84.1 %shard_map.121 = (f32[128,384]{1,0:T(8,128)}, f32[128,384]{1,0:T(8,128)}, f32[8,128]{1,0:T(8,128)}) custom-call(bf16[1024,384]{1,0:T(8,128)(2,1)} %copy.19.x_ref, bf16[384,1024]{1,0:T(8,128)(2,1)} %convert_bitcast_fusion.1.xt_ref, bf16[1024,384]{1,0:T(8,128)(2,1)} %copy.20.d_ref, bf16[384,1024]{1,0:T(8,128)(2,1)} %get-tuple-element.13.dt_ref, ...), custom_call_target="tpu_custom_call" | custom-call | tf_op jit(solution)/shard_map/pallas_call | solution.py:338
  150.3 1.2 slice_bitcast_fusion
  151.5 0.0 copy-start.3
  151.5 0.0 copy-start.2
  151.5 1.5 copy.23
  152.9 0.0 copy-done.3
  152.9 0.7 copy.33
  153.6 0.0 copy-done.2
  153.6 0.7 copy.34
  (6 shorter events, 0.0 us)
Async XLA Ops:
  0.6 3.1 %copy-start.5 = (f32[384]{0:T(512)S(1)}, f32[384]{0:T(512)}, u32[]{:S(2)}) copy-start(f32[384]{0:T(512)} %param.14) | copy-start | bytes 4612
  0.6 3.1 %copy-start.6 = (f32[384]{0:T(512)S(1)}, f32[384]{0:T(512)}, u32[]{:S(2)}) copy-start(f32[384]{0:T(512)} %param.15) | copy-start | bytes 4612
  0.7 3.1 %copy-start.7 = (f32[384]{0:T(512)S(1)}, f32[384]{0:T(512)}, u32[]{:S(2)}) copy-start(f32[384]{0:T(512)} %param.13) | copy-start | bytes 4612
  33.8 1.3 copy-start.1
  34.8 0.7 copy-start.4
  35.6 15.6 %copy-start = (f32[48,8,8,128]{3,2,1,0:T(8,128)}, f32[48,8,8,128]{3,2,1,0:T(8,128)S(1)}, u32[]{:S(2)}) copy-start(f32[48,8,8,128]{3,2,1,0:T(8,128)S(1)} %convert.3) | copy-start | bytes 4718596
  54.7 2.5 %copy-start.8 = (s32[8,128]{1,0:T(8,128)S(1)}, s32[8,128]{1,0:T(8,128)}, u32[]{:S(2)}) copy-start(s32[8,128]{1,0:T(8,128)} %param.12) | copy-start | bytes 12292
  151.5 1.5 copy-start.3
  151.5 2.2 %copy-start.2 = (f32[128,384]{1,0:T(8,128)S(1)}, f32[128,384]{1,0:T(8,128)}, u32[]{:S(2)}) copy-start(f32[128,384]{1,0:T(8,128)} %get-tuple-element.21) | copy-start | bytes 589828

commit v3 on v2

--- a/solution.py
+++ b/solution.py
@@ -9,7 +9,7 @@
 
 SUB = 3
 BATCHES = 64
-CHUNKS = 4
+ACROSS_FIRST = ()
 MESH = pl.DeviceIdType.MESH
 F32 = jnp.float32
 BF16 = jnp.bfloat16
@@ -151,31 +151,65 @@
     return tree(parts[::2]) + tree(parts[1::2])
 
 
+def chunk_count(block):
+    return 8 if block % 64 == 0 else 4
+
+
+def orders(chunks):
+    plan = {}
+    for c in range(chunks):
+        for m in range(2):
+            plane = "qa" if m == 0 else "aq"
+            plan[m, c] = "z" + plane if c in ACROSS_FIRST else plane + "z"
+    return plan
+
+
+def layout(zs, bs, chunks):
+    size = {"z": zs, "a": bs // 4, "q": 2}
+    groups = {}
+    for key, order in sorted(orders(chunks).items()):
+        groups.setdefault(order, []).append(key)
+    shapes = []
+    for order, members in sorted(groups.items()):
+        left = "zaq"
+        for axis in order:
+            left = left.replace(axis, "")
+            shapes.append((order, (len(members), size[axis] - 1) + tuple(size[k] for k in left)))
+    return groups, shapes
+
+
 def backward_kernel(
-    zs, bs, gathered,
-    x_ref, xt_ref, d_ref, dt_ref, wi_ref, wo_ref, loss_ref,
+    zs, bs, chunks, gathered,
+    x_ref, d_ref, wi_ref, wo_ref, loss_ref,
     gin_ref, gout_ref, total_ref,
-    g0, g1, c0, c1, q0, q1, a0, a1, z0, z1, lc, lq, la, lz,
-    send, recv, lsend, lrecv,
+    g0, g1, c0, c1, lc, lq, la, lz,
+    send, recv, lsend, lrecv, *stages,
 ):
     quads = bs // 4
+    size = {"z": zs, "a": quads, "q": 2}
     me_z, me_b = lax.axis_index("bx"), lax.axis_index("by")
     core, q, a = lax.rem(me_b, 2), lax.rem(me_b // 2, 2), me_b // 4
+    mine = {"z": me_z, "a": a, "q": q}
     rows, feats = g0.shape[-2:]
-    grads, cores, qs, quadss, zz = (g0, g1), (c0, c1), (q0, q1), (a0, a1), (z0, z1)
+    grads, cores = (g0, g1), (c0, c1)
     outs = (gout_ref, gin_ref)
-
-    def other_a(s):
-        return lax.rem(a + s, quads)
-
-    def other_z(s):
-        return lax.rem(me_z + s, zs)
+    plan = orders(chunks)
+    groups, shapes = layout(zs, bs, chunks)
+    landing = {}
+    for (order, _), ref in zip(shapes, stages):
+        landing.setdefault(order, []).append(ref)
+
+    def other(axis, s):
+        return lax.rem(mine[axis] + s, size[axis])
 
     core_peer = (me_z, me_b + 1 - 2 * core)
-    q_peer = (me_z, me_b + 2 - 4 * q)
-    a_peers = [(me_z, other_a(s) * 4 + lax.rem(me_b, 4)) for s in range(1, quads)]
-    z_peers = [(other_z(s), me_b) for s in range(1, zs)]
-    everyone = [core_peer, q_peer] + a_peers + z_peers
+    peers = {
+        "q": [(me_z, me_b + 2 - 4 * q)],
+        "a": [(me_z, other("a", s) * 4 + lax.rem(me_b, 4)) for s in range(1, quads)],
+        "z": [(other("z", s), me_b) for s in range(1, zs)],
+    }
+    everyone = [core_peer] + peers["q"] + peers["a"] + peers["z"]
+    base = {"q": 1, "a": 2, "z": 2 + quads - 1}
 
     barrier = pltpu.get_barrier_semaphore()
     for peer in everyone:
@@ -187,27 +221,36 @@
             device_id=peer, device_id_type=MESH,
         )
 
-    kq, ka, kz = 1, 2, 2 + quads - 1
+    def held(stage, m, c):
+        if stage == 1:
+            return cores[m], (c,), "zaq"
+        order = plan[m, c]
+        left = "".join(k for k in "zaq" if k not in order[: stage - 1])
+        return landing[order][stage - 2], (groups[order].index((m, c)), 0), left
+
+    def part(lead, left, axis, at):
+        return lead + tuple(at if k == axis else slice(None) for k in left)
 
     def copies(stage, m, c):
-        def one(src, dst, peer, k):
-            return remote(src, dst, peer, send.at[c, m, k], recv.at[c, m, k])
-
         if stage == 0:
-            return [one(grads[m].at[c, :, :, :, 1 - core], cores[m].at[c], core_peer, 0)]
-        if stage == 3:
-            held = a0.at[c, 0] if m == 0 else q1.at[c]
             return [
-                one(held.at[other_z(s)], zz[m].at[c, s - 1], z_peers[s - 1], kz + s - 1)
-                for s in range(1, zs)
+                remote(
+                    grads[m].at[c, :, :, :, 1 - core], cores[m].at[c], core_peer,
+                    send.at[c, m, 0], recv.at[c, m, 0],
+                )
             ]
-        if (m == 0) == (stage == 1):
-            src = c0.at[c, :, :, 1 - q] if m == 0 else a1.at[c, 0, :, 1 - q]
-            return [one(src, qs[m].at[c], q_peer, kq)]
-        held = q0 if m == 0 else c1
+        order = plan[m, c]
+        axis = order[stage - 1]
+        ref, lead, left = held(stage, m, c)
+        spot = groups[order].index((m, c))
         return [
-            one(held.at[c, :, other_a(s)], quadss[m].at[c, s - 1], a_peers[s - 1], ka + s - 1)
-            for s in range(1, quads)
+            remote(
+                ref.at[part(lead, left, axis, other(axis, s))],
+                landing[order][stage - 1].at[spot, s - 1],
+                peers[axis][s - 1],
+                send.at[c, m, base[axis] + s - 1], recv.at[c, m, base[axis] + s - 1],
+            )
+            for s in range(1, size[axis])
         ]
 
     def gather_sum(stage, m, c):
@@ -215,42 +258,53 @@
             @pl.loop(0, zs)
             def _(z):
                 cores[m][c, z] = cores[m][c, z] + grads[m][c, z, :, :, core]
-        elif stage == 3:
-            own = a0[c, 0, me_z] if m == 0 else q1[c, me_z]
-            outs[m][c * rows:(c + 1) * rows] = tree(
-                [own] + [zz[m][c, s] for s in range(zs - 1)]
-            )
-        elif (m == 0) == (stage == 1):
-            own = c0[c, :, :, q] if m == 0 else a1[c, 0, :, q]
-            qs[m][c] = qs[m][c] + own
+            return
+        order = plan[m, c]
+        axis = order[stage - 1]
+        ref, lead, left = held(stage, m, c)
+        spot = groups[order].index((m, c))
+        came = landing[order][stage - 1]
+        summed = tree(
+            [ref[part(lead, left, axis, mine[axis])]]
+            + [came[spot, s] for s in range(size[axis] - 1)]
+        )
+        if stage == 3:
+            outs[m][c * rows:(c + 1) * rows] = summed
         else:
-            own = q0[c, :, a] if m == 0 else c1[c, :, a]
-            quadss[m][c, 0] = tree([own] + [quadss[m][c, s] for s in range(quads - 1)])
+            came[spot, 0] = summed
+
+    loss_axes = "qaz"
+    loss_from = [loss_ref, lc, lq.at[0], la.at[0]]
+    loss_into = [lc, lq, la, lz]
 
     def loss_copies(stage):
         if stage == 0:
             return [remote(loss_ref, lc, core_peer, lsend.at[0], lrecv.at[0])]
-        if stage == 1:
-            return [remote(lc, lq, q_peer, lsend.at[1], lrecv.at[1])]
-        if stage == 2:
-            return [
-                remote(lq, la.at[s - 1], a_peers[s - 1], lsend.at[ka + s - 1], lrecv.at[ka + s - 1])
-                for s in range(1, quads)
-            ]
+        axis = loss_axes[stage - 1]
         return [
-            remote(la.at[0], lz.at[s - 1], z_peers[s - 1], lsend.at[kz + s - 1], lrecv.at[kz + s - 1])
-            for s in range(1, zs)
+            remote(
+                loss_from[stage], loss_into[stage].at[s - 1], peers[axis][s - 1],
+                lsend.at[base[axis] + s - 1], lrecv.at[base[axis] + s - 1],
+            )
+            for s in range(1, size[axis])
         ]
 
     def loss_sum(stage):
         if stage == 0:
             lc[...] = lc[...] + loss_ref[...]
-        elif stage == 1:
-            lq[...] = lq[...] + lc[...]
-        elif stage == 2:
-            la[0] = tree([lq[...]] + [la[s] for s in range(quads - 1)])
+            return
+        came = loss_into[stage]
+        summed = tree(
+            [loss_from[stage][...]]
+            + [came[s] for s in range(size[loss_axes[stage - 1]] - 1)]
+        )
+        if stage == 3:
+            total_ref[...] = summed
         else:
-            total_ref[...] = tree([la[0]] + [lz[s] for s in range(zs - 1)])
+            came[0] = summed
+
+    def transposed_dot(lhs, rhs):
+        return lax.dot_general(lhs, rhs, (((1,), (1,)), ((), ())), preferred_element_type=F32)
 
     def compute(c):
         @pl.loop(0, zs)
@@ -260,13 +314,13 @@
                 wo = wo_ref[pl.ds(z * bs, bs), c].reshape(bs * rows, feats)
             else:
                 wi, wo = wi_ref[c * zs + z], wo_ref[c * zs + z]
-            pre = jnp.dot(wi, xt_ref[...], preferred_element_type=F32)
+            pre = transposed_dot(wi, x_ref[...])
             sig = jax.nn.sigmoid(pre)
             hidden = (pre * sig).astype(BF16)
             g0[c, z] = jnp.dot(hidden, d_ref[...], preferred_element_type=F32).reshape(
                 quads, 2, 2, rows, feats
             )
-            dhid = jnp.dot(wo, dt_ref[...], preferred_element_type=F32)
+            dhid = transposed_dot(wo, d_ref[...])
             dpre = (dhid * sig * (1.0 + pre * (1.0 - sig))).astype(BF16)
             g1[c, z] = jnp.dot(dpre, x_ref[...], preferred_element_type=F32).reshape(
                 quads, 2, 2, rows, feats
@@ -281,8 +335,8 @@
         return group
 
     flying = {}
-    for step in range(CHUNKS + 4):
-        if step < CHUNKS:
+    for step in range(chunks + 4):
+        if step < chunks:
             compute(step)
             if step == 0:
                 pl.semaphore_wait(barrier, len(everyone))
@@ -292,7 +346,7 @@
             flying["loss", 0] = begin(loss_copies(0))
         for stage in range(4):
             c = step - 1 - stage
-            if not 0 <= c < CHUNKS:
+            if not 0 <= c < chunks:
                 continue
             for m in range(2):
                 for copy in flying[stage, m, c]:
@@ -303,58 +357,52 @@
             if c == 0:
                 for copy in flying["loss", stage]:
                     copy.wait_recv()
-                if stage == 2:
-                    loss_sum(stage)
-                    flying["loss", 3] = begin(loss_copies(3))
-                else:
-                    loss_sum(stage)
-                    if stage < 3:
-                        flying["loss", stage + 1] = begin(loss_copies(stage + 1))
+                loss_sum(stage)
+                if stage < 3:
+                    flying["loss", stage + 1] = begin(loss_copies(stage + 1))
     for copy in started:
         copy.wait_send()
 
 
-def backward(x, xt, d, dt, wi, wo, partial_loss):
+def backward(x, d, wi, wo, partial_loss):
     zs, bs = lax.axis_size("bx"), lax.axis_size("by")
     quads = bs // 4
     hid, feats = wo.shape
     blocks = zs * bs
-    rows = hid // blocks // CHUNKS
+    chunks = chunk_count(hid // blocks)
+    rows = hid // blocks // chunks
     gathered = rows % 16 == 0
-    wi = wi.T.reshape(blocks, CHUNKS, rows, feats)
-    wo = wo.reshape(blocks, CHUNKS, rows, feats)
+    wi = wi.T.reshape(blocks, chunks, rows, feats)
+    wo = wo.reshape(blocks, chunks, rows, feats)
     if not gathered:
         wi, wo = (
-            w.transpose(1, 0, 2, 3).reshape(CHUNKS * zs, bs * rows, feats) for w in (wi, wo)
+            w.transpose(1, 0, 2, 3).reshape(chunks * zs, bs * rows, feats) for w in (wi, wo)
         )
     kinds = 2 + (quads - 1) + (zs - 1)
     vmem = pl.BlockSpec(memory_space=pltpu.VMEM)
     tile = partial_loss.shape
 
     def buf(*shape):
-        return pltpu.VMEM((CHUNKS,) + shape + (rows, feats), F32)
-
-    grad = jax.ShapeDtypeStruct((rows * CHUNKS, feats), F32)
+        return pltpu.VMEM(shape + (rows, feats), F32)
+
+    grad = jax.ShapeDtypeStruct((rows * chunks, feats), F32)
     return pl.pallas_call(
-        functools.partial(backward_kernel, zs, bs, gathered),
+        functools.partial(backward_kernel, zs, bs, chunks, gathered),
         out_shape=(grad, grad, jax.ShapeDtypeStruct(tile, F32)),
-        in_specs=[vmem] * 7,
+        in_specs=[vmem] * 5,
         out_specs=(vmem,) * 3,
         scratch_shapes=[
-            buf(zs, quads, 2, 2), buf(zs, quads, 2, 2),
-            buf(zs, quads, 2), buf(zs, quads, 2),
-            buf(zs, quads), buf(zs),
-            buf(quads - 1, zs), buf(quads - 1, zs, 2),
-            buf(zs - 1), buf(zs - 1),
-            pltpu.VMEM(tile, F32), pltpu.VMEM(tile, F32),
+            buf(chunks, zs, quads, 2, 2), buf(chunks, zs, quads, 2, 2),
+            buf(chunks, zs, quads, 2), buf(chunks, zs, quads, 2),
+            pltpu.VMEM(tile, F32), pltpu.VMEM((1,) + tile, F32),
             pltpu.VMEM((quads - 1,) + tile, F32), pltpu.VMEM((zs - 1,) + tile, F32),
-            pltpu.SemaphoreType.DMA((CHUNKS, 2, kinds)),
-            pltpu.SemaphoreType.DMA((CHUNKS, 2, kinds)),
+            pltpu.SemaphoreType.DMA((chunks, 2, kinds)),
+            pltpu.SemaphoreType.DMA((chunks, 2, kinds)),
             pltpu.SemaphoreType.DMA((kinds,)),
             pltpu.SemaphoreType.DMA((kinds,)),
-        ],
+        ] + [buf(*shape) for _, shape in layout(zs, bs, chunks)[1]],
         compiler_params=pltpu.CompilerParams(collective_id=0, has_side_effects=True),
-    )(x, xt, d, dt, wi, wo, partial_loss)
+    )(x, d, wi, wo, partial_loss)
 
 
 def on_device(state, target, land_mask, batch_map, diffusion, speed_x, speed_y, w_in, w_out):
@@ -364,7 +412,6 @@
     total = local_cols * lax.axis_size("bx") * lax.axis_size("by")
     flat = field.reshape(local_cols, feats)
     x = flat.astype(BF16)
-    xt = x.T
     pre = jnp.dot(x, w_in, preferred_element_type=F32)
     hidden = jax.nn.silu(pre).astype(BF16)
     tend = jnp.dot(hidden, w_out, preferred_element_type=F32)
@@ -381,7 +428,7 @@
     )
     d = (err * total ** (-0.5)).astype(BF16)
     grad_in, grad_out, loss = backward(
-        x, xt, d, d.T, w_in, w_out, jnp.broadcast_to(partial_loss[None, :], (8, width))
+        x, d, w_in, w_out, jnp.broadcast_to(partial_loss[None, :], (8, width))
     )
     return (new_state, grad_in, grad_out, loss[0, :BATCHES])
 

time: 155 us -> 141 us (0.910)
  Pallas kernels: 112 us -> 104 us
  other arithmetic: 6.43 us -> 2.93 us
    pallas_call x1, Pallas kernels: 84.1 us -> 76.2 us  [backward(): pl.pallas_call(functools.partial(backward_kernel, zs, bs, chunks, gathere...]
    unnamed x22 -> x14, local copies, waits for them, and re-layouts: 6.47 us -> 10.1 us
    reduce_sum x1 -> x0, other arithmetic: 3.55 us -> none  [on_device(): persq = 0.5 * jnp.sum(err * err, axis=1)]
    convert_element_type x2 -> x1, local copies, waits for them, and re-layouts: 4.77 us -> 1.63 us  [on_device(): err = weights * (tend - target.reshape(feats, local_cols).T.astype(F32))]
    another operation x3, local copies, waits for them, and re-layouts: 0.01 us -> 2.05 us  [transported(): jnp.stack([diffusion, speed_x, speed_y])]
    reshape x1 -> x0, local copies, waits for them, and re-layouts: 1.87 us -> none  [on_device(): flat = field.reshape(local_cols, feats)]
    transpose x1, local copies, waits for them, and re-layouts: 4.63 us -> 2.79 us  [backward(): wi = wi.T.reshape(blocks, chunks, rows, feats)]
where the time goes in v3:
time: 141 us; the launch traced here: 140 us
  Pallas kernels  104 us (74%)
  local copies, waits for them, and re-layouts  18.5 us (13%)
  matrix products  14.7 us (10%)
  other arithmetic  2.93 us (2%)
    pallas_call x1, Pallas kernels, backward(): pl.pallas_call(functools.partial(backward_kernel, zs, bs, chunks, gathere...  76.2 us
    pallas_call x1, Pallas kernels, transported(): pl.pallas_call(functools.partial(halo_kernel, zs, bs), out_shape=jax.Shap...  27.4 us
    dot_general x1, matrix products, on_device(): tend = jnp.dot(hidden, w_out, preferred_element_type=F32)  14.4 us
    unnamed x14, local copies, waits for them, and re-layouts  10.1 us

profile of v3, /device:TPU:0, one launch (start us, length us, event | category | flops | bytes accessed | tf_op | source)
XLA Modules:
  0.0 140.5 jit_solution(2948945458373885781)
XLA Ops:
  0.6 0.1 pad.3.clone
  0.7 0.7 stack.9
  1.4 0.7 stack.10
  2.1 0.7 stack.11
  2.8 0.7 convert_bitcast_fusion
  3.5 0.7 maximum_maximum_fusion.coef
  4.1 3.0 %copy.13 = f32[384,8,128]{0,2,1:T(8,128)} copy(f32[384,8,128]{2,1,0:T(8,128)} %param.9) | data formatting | bytes 3145728 | tf_op args[0]
  7.1 27.4 %shard_map.120 = f32[8,128,384]{2,1,0:T(8,128)} custom-call(f32[8,128,384]{2,1,0:T(8,128)} %bitcast.35, f32[8,384]{1,0:T(8,128)} %maximum_maximum_fusion.coef), custom_call_target="tpu_custom_call" | custom-call | tf_op jit(solution)/shard_map/pallas_call | solution.py:135
  34.6 0.0 copy-start.3
  34.6 1.6 %bitcast_convert_fusion.x_ref = bf16[1024,384]{1,0:T(8,128)(2,1)S(1)} fusion(f32[8,128,384]{2,1,0:T(8,128)} %shard_map.120), kind=kLoop, calls=%fused_computation.6 | loop fusion | flops 393216 | bytes 2359296 | tf_op jit(solution)/shard_map/convert_element_type | solution.py:414
  36.2 0.0 copy-done.3
  36.2 0.0 copy-start.2
  36.2 0.0 copy-start
  36.2 1.6 %copy.14 = f32[384,8,128]{0,2,1:T(8,128)} copy(bf16[384,8,128]{2,1,0:T(8,128)(2,1)S(1)} %copy-done.3) | data formatting | bytes 2359296 | tf_op jit(solution)/shard_map/convert_element_type | solution.py:419
  37.8 0.6 copy-done
  38.5 0.0 copy-start.4
  38.5 14.4 %multiply_reduce_fusion = (f32[1024]{0:T(1024)S(1)}, bf16[1024,384]{1,0:T(8,128)(2,1)}, f32[1024,384]{1,0:T(8,128)}) fusion(f32[384,8,128]{0,2,1:T(8,128)} %copy.14, f32[1024]{0:T(1024)S(1)} %convert_bitcast_fusion, f32[8,128,384]{2,1,0:T(8,128)S(1)} %copy-done, bf16[4096,384]{1,0:T(8,128)(2,1)} %param.17, ...), kind=kOutput, calls=%fused_computation.7 | convolution fusion | flops 6466960384 | bytes 12591104 | tf_op jit(solution)/shard_map/dot_general | solution.py:417
  52.8 0.0 copy-done.2
  52.8 0.0 copy-done.4
  52.9 0.4 fusion.4
  53.2 0.6 broadcast_in_dim.5.loss_ref
  53.8 0.0 copy-start.1
  53.8 3.2 %copy.16 = f32[384,8,128]{2,1,0:T(8,128)} copy(f32[384,8,128]{0,2,1:T(8,128)} %bitcast.38) | data formatting | bytes 3145728
  57.0 0.0 copy-done.1
  57.0 2.8 %copy.15 = bf16[4096,384]{1,0:T(8,128)(2,1)} copy(bf16[4096,384]{0,1:T(8,128)(2,1)S(1)} %bitcast.37) | data formatting | bytes 6291456 | tf_op jit(solution)/shard_map/transpose | solution.py:375
  59.8 76.2 %shard_map.121 = (f32[128,384]{1,0:T(8,128)}, f32[128,384]{1,0:T(8,128)}, f32[8,128]{1,0:T(8,128)}) custom-call(bf16[1024,384]{1,0:T(8,128)(2,1)} %copy-done.2, bf16[1024,384]{1,0:T(8,128)(2,1)} %get-tuple-element.15.d_ref, bf16[32,8,16,384]{3,2,1,0:T(8,128)(2,1)} %bitcast.34, bf16[32,8,16,384]{3,2,1,0:T(8,128)(2,1)} %bitcast.36, ...), custom_call_target="tpu_custom_call" | custom-call | tf_op jit(solution)/shard_map/pallas_call | solution.py:389
  136.1 1.2 slice_bitcast_fusion
  137.3 1.6 %copy.19 = f32[128,384]{1,0:T(8,128)} copy(f32[128,384]{1,0:T(8,128)} %get-tuple-element.22) | data formatting | bytes 393216
  138.9 1.6 %copy.20 = f32[128,384]{1,0:T(8,128)} copy(f32[128,384]{1,0:T(8,128)} %get-tuple-element.23) | data formatting | bytes 393216
  (2 shorter events, 0.0 us)
Async XLA Ops:
  34.6 1.6 %copy-start.3 = (bf16[384,8,128]{2,1,0:T(8,128)(2,1)S(1)}, bf16[384,8,128]{2,1,0:T(8,128)(2,1)}, u32[]{:S(2)}) copy-start(bf16[384,8,128]{2,1,0:T(8,128)(2,1)} %param.10) | copy-start | bytes 2359300
  36.2 16.6 %copy-start.2 = (bf16[1024,384]{1,0:T(8,128)(2,1)}, bf16[1024,384]{1,0:T(8,128)(2,1)S(1)}, u32[]{:S(2)}) copy-start(bf16[1024,384]{1,0:T(8,128)(2,1)S(1)} %bitcast_convert_fusion.x_ref) | copy-start | bytes 2359300
  36.2 2.3 %copy-start = (f32[8,128,384]{2,1,0:T(8,128)S(1)}, f32[8,128,384]{2,1,0:T(8,128)}, u32[]{:S(2)}) copy-start(f32[8,128,384]{2,1,0:T(8,128)} %shard_map.120) | copy-start | bytes 4718596
  38.5 14.4 %copy-start.4 = (s32[8,128]{1,0:T(8,128)S(1)}, s32[8,128]{1,0:T(8,128)}, u32[]{:S(2)}) copy-start(s32[8,128]{1,0:T(8,128)} %param.12) | copy-start | bytes 12292
  53.8 3.2 %copy-start.1 = (bf16[384,4096]{1,0:T(8,128)(2,1)S(1)}, bf16[384,4096]{1,0:T(8,128)(2,1)}, u32[]{:S(2)}) copy-start(bf16[384,4096]{1,0:T(8,128)(2,1)} %param.16) | copy-start | bytes 9437188

commit v4 on v3

--- a/solution.py
+++ b/solution.py
@@ -20,7 +20,7 @@
 SIDES = [(dx, dy) for dx in (-1, 0, 1) for dy in (-1, 0, 1) if dx or dy]
 
 
-def halo_kernel(zs, bs, cells, coef, out, first, second, send, recv):
+def halo_kernel(zs, bs, cells, kap_ref, sx_ref, sy_ref, out, out_x, first, second, send, recv):
     rows, depth, feats = cells.shape
     me_z, me_b = lax.axis_index("bx"), lax.axis_index("by")
     window = pl.ds(EDGE, depth)
@@ -88,7 +88,7 @@
         def _():
             copy_to(side).wait_send()
 
-    kap, sxx, syy = coef[0:1], coef[1:2], coef[2:3]
+    kap, sxx, syy = kap_ref[...], sx_ref[...], sy_ref[...]
     low = jnp.where(me_b > 0, 1.0, 0.0).astype(F32)
     high = jnp.where(me_b < bs - 1, 1.0, 0.0).astype(F32)
 
@@ -112,7 +112,9 @@
         @pl.loop(SUB - margin, SUB + rows + margin)
         def _(i):
             if margin == 0:
-                out[i - SUB] = moved(src, i, EDGE, depth)
+                value = moved(src, i, EDGE, depth)
+                out[i - SUB] = value
+                out_x[i - SUB] = value.astype(BF16)
             else:
                 at = me_z * rows + i - SUB
                 inside = jnp.where((at >= 0) & (at < rows * zs), 1.0, 0.0).astype(F32)
@@ -127,22 +129,21 @@
     zs, bs = lax.axis_size("bx"), lax.axis_size("by")
     cells = state.transpose(1, 2, 0)
     rows, depth, feats = cells.shape
-    coef = jnp.concatenate(
-        [jnp.stack([diffusion, speed_x, speed_y]), jnp.zeros((5, feats), F32)], axis=0
-    )
     vmem = pl.BlockSpec(memory_space=pltpu.VMEM)
     padded = pltpu.VMEM((rows + 2 * SUB, depth + 2 * EDGE, feats), F32)
     return pl.pallas_call(
         functools.partial(halo_kernel, zs, bs),
-        out_shape=jax.ShapeDtypeStruct(cells.shape, F32),
-        in_specs=[vmem] * 2,
-        out_specs=vmem,
+        out_shape=(
+            jax.ShapeDtypeStruct(cells.shape, F32), jax.ShapeDtypeStruct(cells.shape, BF16)
+        ),
+        in_specs=[vmem] * 4,
+        out_specs=(vmem,) * 2,
         scratch_shapes=[
             padded, padded,
             pltpu.SemaphoreType.DMA((len(SIDES),)), pltpu.SemaphoreType.DMA((len(SIDES),)),
         ],
         compiler_params=pltpu.CompilerParams(collective_id=1, has_side_effects=True),
-    )(cells, coef)
+    )(cells, diffusion[None, :], speed_x[None, :], speed_y[None, :])
 
 
 def tree(parts):
@@ -407,11 +408,11 @@
 
 def on_device(state, target, land_mask, batch_map, diffusion, speed_x, speed_y, w_in, w_out):
     feats, rows_x, rows_y = state.shape
-    field = transported(state, diffusion, speed_x, speed_y)
+    field, field_x = transported(state, diffusion, speed_x, speed_y)
     local_cols = rows_x * rows_y
     total = local_cols * lax.axis_size("bx") * lax.axis_size("by")
     flat = field.reshape(local_cols, feats)
-    x = flat.astype(BF16)
+    x = field_x.reshape(local_cols, feats)
     pre = jnp.dot(x, w_in, preferred_element_type=F32)
     hidden = jax.nn.silu(pre).astype(BF16)
     tend = jnp.dot(hidden, w_out, preferred_element_type=F32)

time: 141 us -> 141 us (level)
  other arithmetic: 2.93 us -> 0.69 us
  local copies, waits for them, and re-layouts: 18.5 us -> 20.6 us
    broadcast_in_dim x1 -> x3, local copies, waits for them, and re-layouts: 0.01 us -> 3.75 us  [the longest x1 1.26 us: transported(): speed_y[None, :]]
    another operation x3 -> x0, local copies, waits for them, and re-layouts: 2.05 us -> none  [transported(): jnp.stack([diffusion, speed_x, speed_y])]
    convert_element_type x1 -> x0, other arithmetic: 1.57 us -> none  [on_device(): x = flat.astype(BF16)]
    unnamed x14 -> x10, local copies, waits for them, and re-layouts: 10.1 us -> 9.44 us
where the time goes in v4:
time: 141 us
  Pallas kernels  104 us (74%)
  local copies, waits for them, and re-layouts  20.6 us (15%)
  matrix products  14.6 us (10%)
    pallas_call x1, Pallas kernels, backward(): pl.pallas_call(functools.partial(backward_kernel, zs, bs, chunks, gathere...  76.2 us
    pallas_call x1, Pallas kernels, transported(): pl.pallas_call(functools.partial(halo_kernel, zs, bs), out_shape=(jax.Sha...  27.8 us
    dot_general x1, matrix products, on_device(): tend = jnp.dot(hidden, w_out, preferred_element_type=F32)  14.2 us
    unnamed x10, local copies, waits for them, and re-layouts  9.44 us
    convert_element_type x1, local copies, waits for them, and re-layouts, on_device(): err = weights * (tend - target.reshape(feats, local_cols).T.astype(F32))  2.83 us

profile of v4, /device:TPU:0, one launch (start us, length us, event | category | flops | bytes accessed | tf_op | source)
XLA Modules:
  0.0 140.5 jit_solution(14635659496446812536)
XLA Ops:
  0.6 1.2 broadcast_in_dim.8.kap_ref
  1.9 1.2 broadcast_in_dim.18.sx_ref
  3.1 1.3 broadcast_in_dim.19.sy_ref
  4.4 0.7 convert_bitcast_fusion
  5.1 0.0 copy-start
  5.1 3.2 %copy.13 = f32[384,8,128]{0,2,1:T(8,128)} copy(f32[384,8,128]{2,1,0:T(8,128)} %param.9) | data formatting | bytes 3145728 | tf_op args[0]
  8.3 27.8 %shard_map.120 = (f32[8,128,384]{2,1,0:T(8,128)}, bf16[8,128,384]{2,1,0:T(8,128)(2,1)}) custom-call(f32[8,128,384]{2,1,0:T(8,128)} %bitcast.35, f32[1,384]{1,0:T(1,128)} %broadcast_in_dim.8.kap_ref, f32[1,384]{1,0:T(1,128)} %broadcast_in_dim.18.sx_ref, f32[1,384]{1,0:T(1,128)} %broadcast_in_dim.19.sy_ref), custom_call_target="tpu_custom_call" | custom-call | tf_op jit(solution)/shard_map/pallas_call | solution.py:134
  36.0 2.8 %copy.14 = f32[384,8,128]{0,2,1:T(8,128)} copy(bf16[384,8,128]{2,1,0:T(8,128)(2,1)} %param.10) | data formatting | bytes 2359296 | tf_op jit(solution)/shard_map/convert_element_type | solution.py:420
  38.9 0.0 copy-done
  38.9 0.0 copy-start.2
  38.9 14.2 %multiply_reduce_fusion = (f32[1024]{0:T(1024)S(1)}, bf16[1024,384]{1,0:T(8,128)(2,1)}, f32[1024,384]{1,0:T(8,128)}) fusion(f32[384,8,128]{0,2,1:T(8,128)} %copy.14, f32[1024]{0:T(1024)S(1)} %convert_bitcast_fusion, f32[8,128,384]{2,1,0:T(8,128)} %get-tuple-element.9, bf16[4096,384]{1,0:T(8,128)(2,1)S(1)} %copy-done, bf16[1024,384]{1,0:T(8,128)(2,1)} %bitcast.39, ...), kind=kOutput, calls=%fused_computation.6 | convolution fusion | flops 6466960384 | bytes 12591104 | tf_op jit(solution)/shard_map/dot_general | solution.py:418
  53.1 0.0 copy-start.1
  53.1 0.0 copy-done.2
  53.1 0.4 fusion.4
  53.4 0.6 broadcast_in_dim.20.loss_ref
  54.1 3.0 %copy.16 = f32[384,8,128]{2,1,0:T(8,128)} copy(f32[384,8,128]{0,2,1:T(8,128)} %bitcast.38) | data formatting | bytes 3145728
  57.1 0.0 copy-done.1
  57.1 2.8 %copy.15 = bf16[4096,384]{1,0:T(8,128)(2,1)} copy(bf16[4096,384]{0,1:T(8,128)(2,1)S(1)} %bitcast.37) | data formatting | bytes 6291456 | tf_op jit(solution)/shard_map/transpose | solution.py:376
  59.9 76.2 %shard_map.121 = (f32[128,384]{1,0:T(8,128)}, f32[128,384]{1,0:T(8,128)}, f32[8,128]{1,0:T(8,128)}) custom-call(bf16[1024,384]{1,0:T(8,128)(2,1)} %bitcast.40, bf16[1024,384]{1,0:T(8,128)(2,1)} %get-tuple-element.19.d_ref, bf16[32,8,16,384]{3,2,1,0:T(8,128)(2,1)} %bitcast.34, bf16[32,8,16,384]{3,2,1,0:T(8,128)(2,1)} %bitcast.36, ...), custom_call_target="tpu_custom_call" | custom-call | tf_op jit(solution)/shard_map/pallas_call | solution.py:390
  136.1 1.2 slice_bitcast_fusion
  137.3 1.6 %copy.19 = f32[128,384]{1,0:T(8,128)} copy(f32[128,384]{1,0:T(8,128)} %get-tuple-element.26) | data formatting | bytes 393216
  138.9 1.6 %copy.20 = f32[128,384]{1,0:T(8,128)} copy(f32[128,384]{1,0:T(8,128)} %get-tuple-element.27) | data formatting | bytes 393216
  (1 shorter events, 0.0 us)
Async XLA Ops:
  5.1 33.8 %copy-start = (bf16[4096,384]{1,0:T(8,128)(2,1)S(1)}, bf16[4096,384]{1,0:T(8,128)(2,1)}, u32[]{:S(2)}) copy-start(bf16[4096,384]{1,0:T(8,128)(2,1)} %param.17) | copy-start | bytes 9437188
  38.9 14.2 %copy-start.2 = (s32[8,128]{1,0:T(8,128)S(1)}, s32[8,128]{1,0:T(8,128)}, u32[]{:S(2)}) copy-start(s32[8,128]{1,0:T(8,128)} %param.12) | copy-start | bytes 12292
  53.1 4.0 %copy-start.1 = (bf16[384,4096]{1,0:T(8,128)(2,1)S(1)}, bf16[384,4096]{1,0:T(8,128)(2,1)}, u32[]{:S(2)}) copy-start(bf16[384,4096]{1,0:T(8,128)(2,1)} %param.16) | copy-start | bytes 9437188
